TPU v7x, 256 devices: a whole 4x4x8 slice. The times are simulated.
256 devices in a mesh: segment: 32 (over z_hi, y, x), tp: 8 (over z_lo, core).
Axes of the slice: x: 4, y: 4, z: 8 (z_hi: 2, z_lo: 4; z = z_hi * 4 + z_lo), core: 2. Of those that a mesh axis runs over, the one named last changes fastest.
Arguments:
- layer_input: bfloat16 [16384, 1024], P('segment'), may hold values from -6 to 6
- cotangent: bfloat16 [16384, 1024], P('segment'), may hold values from -6 to 6
- norm_gain: float32 [32, 1024], P('segment'), may hold values from 0.5 to 1.5
- qkv_weight: bfloat16 [32, 3, 1024, 1024], P('segment', None, None, 'tp'), may hold values from -0.1875 to 0.1875
- out_weight: bfloat16 [32, 1024, 1024], P('segment', 'tp'), may hold values from -0.1875 to 0.1875
- up_weight: bfloat16 [32, 1024, 4096], P('segment', None, 'tp'), may hold values from -0.1875 to 0.1875
- down_weight: bfloat16 [32, 4096, 1024], P('segment', 'tp'), may hold values from -0.09375 to 0.09375
- logit_scale: float32 [32, 16], P('segment', 'tp'), may hold values from 4 to 16
- neighbour_table: int32 [32, 4, 4], replicated, may hold values from 0 to 3, as said below
- valid_table: int32 [32, 4, 4], replicated, may hold values from 0 to 1
- patch_of_segment: int32 [32], P('segment'), may hold values from 0 to 31, each once
Outputs:
- received: bfloat16 [16384, 1024], P('segment')
- grad_qkv: bfloat16 [32, 3, 1024, 1024], P('segment', None, None, 'tp')
- grad_out: bfloat16 [32, 1024, 1024], P('segment', 'tp')
- grad_up: bfloat16 [32, 1024, 4096], P('segment', None, 'tp')
- grad_down: bfloat16 [32, 4096, 1024], P('segment', 'tp')
- grad_gain: float32 [32, 1024], P('segment')
- grad_scale: float32 [32, 16], P('segment', 'tp')
Inputs may be any that keep to these rules, and one draw needn't show every extreme that they name: `neighbour_table`: in every patch, slot 0 of block b names b itself; the other slots of a block name distinct other blocks of the same patch. `patch_of_segment`: each segment works on a different patch.
All inputs are finite; a program needn't handle non-finite values.
Results may differ from a plain program's by a relative error of at most 0.013.
Values may be sent and summed in bfloat16 or wider, within the bound.
A program may use at most 64 MiB of HBM per device.

v0:
```python
import jax
import jax.numpy as jnp
from jax import lax
from jax.sharding import PartitionSpec as P

BLK = 128


root_half = 0.7071067811865476
normal_peak = 0.3989422804014327


def in_blocks(value, dim, devices):
    lengths = value.shape
    pieces = value.reshape(*lengths[:dim], devices, lengths[dim] // devices, *lengths[dim + 1 :])
    return jnp.moveaxis(pieces, dim, 0)


def summed_on_arrival(value, axis, dim):
    devices = lax.axis_size(axis)
    pieces = lax.all_to_all(in_blocks(value, dim, devices), axis, 0, 0, tiled=True)
    return jnp.sum(pieces.astype(jnp.float32), axis=0)


def from_everyone(value, axis):
    copies = jnp.broadcast_to(value, (lax.axis_size(axis), *value.shape))
    return lax.all_to_all(copies, axis, split_axis=0, concat_axis=0, tiled=True)


def taken_together(value, axis):
    return from_everyone(value, axis).sum(axis=0)


def from_behind(value, axis, by):
    devices = lax.axis_size(axis)
    return lax.ppermute(value, axis, [(i, (i + by) % devices) for i in range(devices)])


def joined_along(pieces, dim):
    lengths = list(pieces.shape[1:])
    lengths[dim] *= pieces.shape[0]
    return jnp.moveaxis(pieces, 0, dim).reshape(lengths)


def gathered_copies(value, axis, dim):
    return joined_along(from_everyone(value, axis), dim)


def batched_product(form, left, right):
    return jnp.einsum(form, left, right, preferred_element_type=jnp.float32)


def layer_terms(
    layer_rows,
    grad_rows,
    gain,
    qkv_part,
    out_part,
    up_part,
    down_part,
    scale,
    neighbours,
    valid_slots,
):
    tok_count = layer_rows.shape[0]
    head_count = scale.shape[0]
    col_count = out_part.shape[0]
    head_dim = col_count // head_count
    block_count = tok_count // BLK
    as_float = layer_rows.astype(jnp.float32)
    centred = as_float - jnp.mean(as_float, -1, keepdims=True)
    inv_spread = lax.rsqrt(jnp.mean(centred * centred, -1, keepdims=True) + 1e-05)
    standard = centred * inv_spread
    unit_scaled = (standard * gain).astype(jnp.bfloat16)
    projected = [
        jnp.dot(unit_scaled, qkv_part[member], preferred_element_type=jnp.float32)
        for member in range(3)
    ]
    raw_query = projected[0].reshape(tok_count, head_count, head_dim)
    raw_key = projected[1].reshape(tok_count, head_count, head_dim)
    inv_query = lax.rsqrt(jnp.sum(raw_query * raw_query, -1, keepdims=True) + 1e-06)
    inv_key = lax.rsqrt(jnp.sum(raw_key * raw_key, -1, keepdims=True) + 1e-06)
    q_unit = (
        (raw_query * inv_query).astype(jnp.bfloat16).reshape(block_count, BLK, head_count, head_dim)
    )
    k_unit = (
        (raw_key * inv_key).astype(jnp.bfloat16).reshape(block_count, BLK, head_count, head_dim)
    )
    values = projected[2].astype(jnp.bfloat16).reshape(block_count, BLK, head_count, head_dim)
    k_near = k_unit[neighbours]
    v_near = values[neighbours]
    cosine = batched_product("bihd,bjthd->bhijt", q_unit, k_near)
    scale_b = scale[None, :, None, None, None]
    live_slots = valid_slots.astype(jnp.float32)[:, None, None, :, None]
    exponent = jnp.exp(scale_b * cosine - scale_b) * live_slots
    weights = exponent / jnp.sum(exponent, (3, 4), keepdims=True)
    weights_b = weights.astype(jnp.bfloat16)
    attended = (
        batched_product("bhijt,bjthd->bihd", weights_b, v_near)
        .astype(jnp.bfloat16)
        .reshape(tok_count, col_count)
    )
    pre_act = jnp.dot(unit_scaled, up_part, preferred_element_type=jnp.float32)
    normal_cdf = 0.5 * (1.0 + lax.erf(pre_act * root_half))
    activated = (pre_act * normal_cdf).astype(jnp.bfloat16)
    grad_down = jnp.dot(activated.T, grad_rows, preferred_element_type=jnp.float32).astype(
        jnp.bfloat16
    )
    d_act = jnp.dot(grad_rows, down_part.T, preferred_element_type=jnp.float32)
    slope = normal_cdf + pre_act * jnp.exp(-0.5 * pre_act * pre_act) * normal_peak
    d_pre = (d_act * slope).astype(jnp.bfloat16)
    grad_up = jnp.dot(unit_scaled.T, d_pre, preferred_element_type=jnp.float32).astype(jnp.bfloat16)
    d_normed = jnp.dot(d_pre, up_part.T, preferred_element_type=jnp.float32)
    d_att = jnp.dot(grad_rows, out_part.T, preferred_element_type=jnp.float32).astype(jnp.bfloat16)
    grad_out = jnp.dot(attended.T, grad_rows, preferred_element_type=jnp.float32).astype(
        jnp.bfloat16
    )
    d_att_blocks = d_att.reshape(block_count, BLK, head_count, head_dim)
    d_weights = batched_product("bihd,bjthd->bhijt", d_att_blocks, v_near)
    inner_sum = jnp.sum(weights * d_weights, (3, 4), keepdims=True)
    d_score = weights * (d_weights - inner_sum)
    grad_scale = jnp.sum(d_score * cosine, (0, 2, 3, 4))
    d_cos = (d_score * scale_b).astype(jnp.bfloat16)
    d_q_unit = batched_product("bhijt,bjthd->bihd", d_cos, k_near).reshape(
        tok_count, head_count, head_dim
    )
    key_terms = batched_product("bhijt,bihd->bjthd", d_cos, q_unit)
    value_terms = batched_product("bhijt,bihd->bjthd", weights_b, d_att_blocks)
    one_hot = (
        neighbours[:, :, None] == jnp.arange(block_count, dtype=jnp.int32)[None, None, :]
    ).astype(jnp.float32)
    d_k_unit = jnp.einsum("bjm,bjthd->mthd", one_hot, key_terms).reshape(
        tok_count, head_count, head_dim
    )
    d_values = jnp.einsum("bjm,bjthd->mthd", one_hot, value_terms).reshape(tok_count, col_count)
    d_raw_query = (
        inv_query * d_q_unit
        - inv_query**3 * jnp.sum(d_q_unit * raw_query, -1, keepdims=True) * raw_query
    )
    d_raw_key = (
        inv_key * d_k_unit - inv_key**3 * jnp.sum(d_k_unit * raw_key, -1, keepdims=True) * raw_key
    )
    d_raw = jnp.stack(
        [
            d_raw_query.reshape(tok_count, col_count),
            d_raw_key.reshape(tok_count, col_count),
            d_values,
        ]
    ).astype(jnp.bfloat16)
    grad_qkv = jnp.stack(
        [
            jnp.dot(unit_scaled.T, d_raw[member], preferred_element_type=jnp.float32)
            for member in range(3)
        ]
    ).astype(jnp.bfloat16)
    for member in range(3):
        d_normed = d_normed + jnp.dot(
            d_raw[member], qkv_part[member].T, preferred_element_type=jnp.float32
        )
    return (d_normed, standard, inv_spread, grad_qkv, grad_out, grad_up, grad_down, grad_scale)


def norm_back(d_normed, grad_rows, standard, inv_spread, gain):
    scaled = d_normed * gain
    first_mean = jnp.mean(scaled, -1, keepdims=True)
    second_mean = jnp.mean(scaled * standard, -1, keepdims=True)
    d_input = (
        grad_rows.astype(jnp.float32) + inv_spread * (scaled - first_mean - standard * second_mean)
    ).astype(jnp.bfloat16)
    gain_grad = jnp.sum(d_normed * standard, 0)
    return (d_input, gain_grad)


def shards(
    layer_input,
    cotangent,
    norm_gain,
    qkv_weight,
    out_weight,
    up_weight,
    down_weight,
    logit_scale,
    neighbour_table,
    valid_table,
    patch_of_segment,
):
    patch_count = neighbour_table.shape[0]
    picked_slots = (jnp.arange(patch_count, dtype=jnp.int32) == patch_of_segment[0]).astype(
        jnp.int32
    )
    neighbours = jnp.sum(picked_slots[:, None, None] * neighbour_table, 0)
    valid_slots = jnp.sum(picked_slots[:, None, None] * valid_table, 0)
    gain = norm_gain[0]
    terms = layer_terms(
        layer_input,
        cotangent,
        gain,
        qkv_weight[0],
        out_weight[0],
        up_weight[0],
        down_weight[0],
        logit_scale[0],
        neighbours,
        valid_slots,
    )
    d_normed, standard, inv_spread, grad_qkv, grad_out, grad_up, grad_down, grad_scale = terms
    row_count = layer_input.shape[0] // lax.axis_size("tp")
    row_start = lax.axis_index("tp") * row_count
    share = summed_on_arrival(d_normed.astype(jnp.bfloat16), "tp", 0)
    grad_share = lax.dynamic_slice_in_dim(cotangent, row_start, row_count, 0)
    standard_share = lax.dynamic_slice_in_dim(standard, row_start, row_count, 0)
    spread_share = lax.dynamic_slice_in_dim(inv_spread, row_start, row_count, 0)
    input_share, gain_part = norm_back(share, grad_share, standard_share, spread_share, gain)
    gain_grad = taken_together(gain_part, "tp")
    shifted = from_behind(input_share, "segment", -1)
    received = gathered_copies(shifted, "tp", 0)
    return (
        received,
        grad_qkv[None],
        grad_out[None],
        grad_up[None],
        grad_down[None],
        gain_grad[None],
        grad_scale[None],
    )


def solution(mesh):
    placed = (
        P("segment", None),
        P("segment", None),
        P("segment", None),
        P("segment", None, None, "tp"),
        P("segment", "tp", None),
        P("segment", None, "tp"),
        P("segment", "tp", None),
        P("segment", "tp"),
        P(),
        P(),
        P("segment"),
    )
    return jax.shard_map(
        shards,
        mesh=mesh,
        in_specs=placed,
        out_specs=(
            P("segment", None),
            P("segment", None, None, "tp"),
            P("segment", "tp", None),
            P("segment", None, "tp"),
            P("segment", "tp", None),
            P("segment", None),
            P("segment", "tp"),
        ),
        check_vma=False,
    )
```

profile of v0, /device:TPU:1, one launch (start us, length us, event | category | flops | bytes accessed | tf_op | source)
XLA Modules:
  0.0 123.5 jit_solution(8148612729862999468)
XLA Ops:
  1.5 1.4 %convert_reduce_fusion = f32[512]{0:T(512)S(1)} fusion(bf16[512,1024]{1,0:T(8,128)(2,1)} %param.11), kind=kLoop, calls=%fused_computation.3 | loop fusion | flops 1048064 | bytes 1050624 | tf_op jit(solution)/shard_map/reduce_sum | solution.py:71
  2.9 1.6 %fusion.2 = f32[512]{0:T(512)S(1)} fusion(bf16[512,1024]{1,0:T(8,128)(2,1)} %param.11, f32[512]{0:T(512)S(1)} %broadcast_multiply_fusion), kind=kLoop, calls=%fused_computation.6 | loop fusion | flops 2096640 | bytes 1052672 | tf_op jit(solution)/shard_map/reduce_sum | solution.py:72
  6.8 1.1 slice_bitcast_fusion.1
  8.0 0.8 copy.86
  8.8 1.7 %fusion = (f32[512,1024]{1,0:T(8,128)}, bf16[512,1024]{1,0:T(8,128)(2,1)S(1)}) fusion(bf16[512,1024]{1,0:T(8,128)(2,1)S(1)} %copy-done.1, f32[512]{0:T(512)S(1)} %add_rsqrt_fusion.2, f32[512]{0:T(512)S(1)} %broadcast_multiply_fusion, f32[1024]{0:T(1024)S(1)} %bitcast.180), kind=kLoop, calls=%fused_computation.4 | loop fusion | flops 2621440 | bytes 4202496 | tf_op jit(solution)/shard_map/mul | solution.py:73
  10.5 1.4 %convolution_convert_fusion.6 = bf16[512,128]{1,0:T(8,128)(2,1)S(1)} fusion(bf16[512,1024]{1,0:T(8,128)(2,1)S(1)} %get-tuple-element.15, bf16[1,3,1024,128]{3,2,1,0:T(8,128)(2,1)} %param.14), kind=kOutput, calls=%fused_computation.40 | convolution fusion | flops 134283264 | bytes 1441792 | tf_op jit(solution)/shard_map/dot_general | solution.py:76
  13.4 1.5 %gather_fusion.1 = bf16[16,128,2,64]{1,3,2,0:T(8,128)(2,1)} fusion(bf16[4,128,2,64]{1,3,2,0:T(8,128)(2,1)S(1)} %copy.92, s32[1024]{0:T(1024)} %pad_clamp_fusion), kind=kCustom, calls=%fused_computation.1 | custom fusion | bytes 1048640 | tf_op jit(solution)/shard_map/gather | solution.py:91
  15.7 1.5 %fusion.4 = (f32[4,2,128]{2,1,0:T(2,128)S(1)}, f32[4,2,128,4,128]{2,4,3,1,0:T(8,128)S(1)}) fusion(f32[4,4]{1,0:T(4,128)} %convert_element_type.88, f32[2]{0:T(128)} %bitcast.184, bf16[4,4,128,2,64]{2,4,3,1,0:T(8,128)(2,1)S(1)} %bitcast.162, bf16[4,128,2,64,1]{1,0,3,2,4:T(4,128)(2,1)S(1)} %bitcast.175), kind=kOutput, calls=%fused_computation.16 | convolution fusion | flops 69204992 | bytes 2756680 | tf_op jit(solution)/shard_map/bihd,bjthd->bhijt/dot_general | solution.py:50
  18.6 0.9 multiply_reduce_fusion.1
  19.5 1.6 %multiply_reduce_fusion = (f32[2]{0:T(128)}, bf16[4,2,128,4,128]{2,4,3,1,0:T(8,128)(2,1)S(1)}) fusion(f32[4,2,128,4,128]{2,4,3,1,0:T(8,128)S(1)} %get-tuple-element.23, f32[4,2,128,4,128]{2,4,3,1,0:T(8,128)S(1)} %get-tuple-element.25, f32[4,2,128]{2,1,0:T(2,128)S(1)} %get-tuple-element.24, f32[4,2,128]{2,1,0:T(2,128)S(1)} %get-tuple-element.22, ...), kind=kLoop, calls=%fused_computation.7 | loop fusion | flops 5242878 | bytes 5251152 | tf_op jit(solution)/shard_map/reduce_sum | solution.py:122
  21.9 1.7 %fusion.20 = f32[512,512]{1,0:T(8,128)} fusion(bf16[512,1024]{1,0:T(8,128)(2,1)S(1)} %get-tuple-element.15, bf16[1,1024,512]{2,1,0:T(8,128)(2,1)S(1)} %copy-done), kind=kOutput, calls=%fused_computation.48 | convolution fusion | flops 536870912 | bytes 3145728 | tf_op jit(solution)/shard_map/dot_general | solution.py:103
  24.5 1.4 %convolution_bitcast_fusion.4 = f32[4,128,2,64]{1,0,3,2:T(4,128)} fusion(bf16[4,4,128,2,64]{2,4,1,3,0:T(8,128)(2,1)S(1)} %convolution_bitcast_fusion.1, s32[4,4]{1,0:T(4,128)S(1)} %copy-done.20), kind=kOutput, calls=%fused_computation.36 | convolution fusion | flops 2097216 | bytes 786496 | tf_op jit(solution)/shard_map/bjm,bjthd->mthd/dot_general | solution.py:132
  25.9 1.1 reshape.203
  27.1 1.5 %fusion.46 = f32[512,1024]{1,0:T(8,128)S(1)} fusion(bf16[512,128]{0,1:T(8,128)(2,1)S(1)} %bitcast.169, bf16[1,3,1024,128]{3,2,1,0:T(8,128)(2,1)} %param.14), kind=kOutput, calls=%fused_computation.79 | convolution fusion | flops 134217728 | bytes 2490368 | tf_op jit(solution)/shard_map/dot_general | solution.py:157
  30.4 1.0 fusion.7
  31.5 1.8 %add_convert_fusion = bf16[512,1024]{1,0:T(8,128)(2,1)} fusion(f32[512,1024]{1,0:T(8,128)S(1)} %fusion.43, f32[512,1024]{1,0:T(8,128)S(1)} %fusion.46, f32[512,1024]{1,0:T(8,128)S(1)} %fusion.41, bf16[512,512]{1,0:T(8,128)(2,1)S(1)} %fusion.7, bf16[1,1024,512]{2,1,0:T(8,128)(2,1)S(1)} %copy-done), kind=kOutput, calls=%fused_computation.9 | convolution fusion | flops 538968064 | bytes 8912896 | tf_op jit(solution)/shard_map/dot_general | solution.py:113
  33.2 7.5 %all-to-all-start = ((bf16[8,64,1024]{2,1,0:T(8,128)(2,1)}), bf16[8,64,1024]{2,1,0:T(8,128)(2,1)}, u32[]{:S(2)}, u32[]{:S(2)}) async-start(bf16[8,64,1024]{2,1,0:T(8,128)(2,1)} %bitcast.164), calls=%async_computation | async-start | bytes 2097152 | tf_op jit(solution)/shard_map/all_to_all | solution.py:21
  41.5 25.1 %all-to-all-done = bf16[8,64,1024]{2,1,0:T(8,128)(2,1)} async-done(((bf16[8,64,1024]{2,1,0:T(8,128)(2,1)}), bf16[8,64,1024]{2,1,0:T(8,128)(2,1)}, u32[]{:S(2)}, u32[]{:S(2)}) %all-to-all-start) | async-done | bytes 1048608 | tf_op jit(solution)/shard_map/all_to_all | solution.py:21
  66.6 1.4 %convert_reduce_fusion.1 = f32[64,1024]{1,0:T(8,128)S(1)} fusion(bf16[8,64,1024]{2,1,0:T(8,128)(2,1)} %all-to-all-done), kind=kLoop, calls=%fused_computation.8 | loop fusion | flops 983040 | bytes 1310720 | tf_op jit(solution)/shard_map/reduce_sum | solution.py:22
  68.1 1.1 multiply_reduce_fusion.2
  69.2 1.1 add_convert_fusion.1
  70.3 9.9 %collective-permute-start = (bf16[64,1024]{1,0:T(8,128)(2,1)S(1)}, bf16[64,1024]{1,0:T(8,128)(2,1)S(1)}, u32[]{:S(2)}, u32[]{:S(2)}) collective-permute-start(bf16[64,1024]{1,0:T(8,128)(2,1)S(1)} %add_convert_fusion.1), channel_id=1, source_target_pairs={{0,248},{8,0},{16,8},{24,16},{32,24},{40,32},{48,40},{56,48},{64,5... | collective-permute-start | bytes 393224 | tf_op jit(solution)/shard_map/ppermute | solution.py:36
  80.2 9.2 %all_to_all.16 = f32[8,1,1024]{2,1,0:T(1,128)} all-to-all(f32[8,1,1024]{2,1,0:T(1,128)S(1)} %broadcast_in_dim.18), channel_id=1, replica_groups=mesh['segment'=32,'tp'=8] {'tp'}, dimensions={0} | all-to-all | bytes 65536 | tf_op jit(solution)/shard_map/all_to_all | solution.py:27
  89.4 1.1 broadcast_in_dim.14
  90.5 4.9 %all-to-all-start.1 = ((bf16[8,64,1024]{2,1,0:T(8,128)(2,1)}), bf16[8,64,1024]{2,1,0:T(8,128)(2,1)}, u32[]{:S(2)}, u32[]{:S(2)}) async-start(bf16[8,64,1024]{2,1,0:T(8,128)(2,1)} %broadcast_in_dim.14), calls=%async_computation.1 | async-start | bytes 2097152 | tf_op jit(solution)/shard_map/all_to_all | solution.py:27
  95.4 2.4 %fusion.14 = bf16[4,128,2,64]{1,3,2,0:T(8,128)(2,1)S(1)} fusion(bf16[4,4,128,2,64]{2,4,3,1,0:T(8,128)(2,1)} %bitcast.165, f32[4,2,128,4,128]{2,4,3,1,0:T(8,128)} %copy-done.6, f32[4,2,128]{2,1,0:T(2,128)S(1)} %copy-done.22, f32[4,4]{1,0:T(4,128)S(1)} %copy-done.15, f32[2]{0:T(128)} %bitcast.185), kind=kOutput, calls=%fused_computation.42 | convolution fusion | flops 69795840 | bytes 2756680 | tf_op jit(solution)/shard_map/bhijt,bjthd->bihd/dot_general | solution.py:50
  99.4 1.0 pad_maximum_fusion
  100.4 1.0 fusion.11
  101.4 1.7 %fusion.5 = bf16[1,1024,512]{2,1,0:T(8,128)(2,1)} fusion(bf16[512,1024]{1,0:T(8,128)(2,1)S(1)} %get-tuple-element.15, bf16[512,512]{1,0:T(8,128)(2,1)S(1)} %copy-done.9), kind=kOutput, calls=%fused_computation.23 | convolution fusion | flops 537395200 | bytes 2621440 | tf_op jit(solution)/shard_map/dot_general | solution.py:112
  103.1 1.7 %fusion.6 = bf16[1,512,1024]{2,1,0:T(8,128)(2,1)} fusion(bf16[512,1024]{1,0:T(8,128)(2,1)S(1)} %copy-done.3, f32[512,512]{1,0:T(8,128)S(1)} %copy-done.26), kind=kOutput, calls=%fused_computation.24 | convolution fusion | flops 538705920 | bytes 3145728 | tf_op jit(solution)/shard_map/dot_general | solution.py:106
  105.5 15.8 %all-to-all-done.1 = bf16[8,64,1024]{2,1,0:T(8,128)(2,1)} async-done(((bf16[8,64,1024]{2,1,0:T(8,128)(2,1)}), bf16[8,64,1024]{2,1,0:T(8,128)(2,1)}, u32[]{:S(2)}, u32[]{:S(2)}) %all-to-all-start.1) | async-done | bytes 1048608 | tf_op jit(solution)/shard_map/all_to_all | solution.py:27
  121.2 2.3 %copy.181 = bf16[512,1024]{1,0:T(8,128)(2,1)} copy(bf16[512,1024]{1,0:T(8,128)(2,1)} %bitcast.38) | data formatting | bytes 2097152
  (97 shorter events, 12.5 us)
Async XLA Ops:
  0.6 21.3 %copy-start = (bf16[1,1024,512]{2,1,0:T(8,128)(2,1)S(1)}, bf16[1,1024,512]{2,1,0:T(8,128)(2,1)}, u32[]{:S(2)}) copy-start(bf16[1,1024,512]{2,1,0:T(8,128)(2,1)} %param.16) | copy-start | bytes 3145732
  0.6 4.0 %copy-start.17 = (s32[32,4,4]{0,2,1:T(4,128)S(1)}, s32[32,4,4]{0,2,1:T(4,128)}, u32[]{:S(2)}) copy-start(s32[32,4,4]{0,2,1:T(4,128)} %param.20) | copy-start | bytes 6148
  0.7 4.0 %copy-start.18 = (s32[32,4,4]{0,2,1:T(4,128)S(1)}, s32[32,4,4]{0,2,1:T(4,128)}, u32[]{:S(2)}) copy-start(s32[32,4,4]{0,2,1:T(4,128)} %param.19) | copy-start | bytes 6148
  0.7 5.5 %copy-start.2 = (bf16[512,1024]{1,0:T(8,128)(2,1)S(1)}, bf16[512,1024]{1,0:T(8,128)(2,1)}, u32[]{:S(2)}) copy-start(bf16[512,1024]{1,0:T(8,128)(2,1)} %param.12) | copy-start | bytes 3145732
  0.7 5.5 %copy-start.10 = (bf16[1,128,1024]{2,1,0:T(8,128)(2,1)S(1)}, bf16[1,128,1024]{2,1,0:T(8,128)(2,1)}, u32[]{:S(2)}) copy-start(bf16[1,128,1024]{2,1,0:T(8,128)(2,1)} %param.15) | copy-start | bytes 786436
  4.6 4.3 %copy-start.1 = (bf16[512,1024]{1,0:T(8,128)(2,1)S(1)}, bf16[512,1024]{1,0:T(8,128)(2,1)}, u32[]{:S(2)}) copy-start(bf16[512,1024]{1,0:T(8,128)(2,1)} %param.11) | copy-start | bytes 3145732
  4.6 4.3 %copy-start.12 = (f32[1,1024]{1,0:T(1,128)S(1)}, f32[1,1024]{1,0:T(1,128)}, u32[]{:S(2)}) copy-start(f32[1,1024]{1,0:T(1,128)} %param.13) | copy-start | bytes 12292
  4.6 5.9 %copy-start.16 = (f32[512]{0:T(512)}, f32[512]{0:T(512)S(1)}, u32[]{:S(2)}) copy-start(f32[512]{0:T(512)S(1)} %add_rsqrt_fusion.2) | copy-start | bytes 6148
  4.9 0.7 copy-start.19
  8.8 3.1 %copy-start.7 = (bf16[128,1024]{1,0:T(8,128)(2,1)S(1)}, bf16[128,1024]{1,0:T(8,128)(2,1)}, u32[]{:S(2)}) copy-start(bf16[128,1024]{1,0:T(8,128)(2,1)} %copy.86) | copy-start | bytes 786436
  15.7 1.5 %copy-start.14 = (f32[4,4]{1,0:T(4,128)S(1)}, f32[4,4]{1,0:T(4,128)}, u32[]{:S(2)}) copy-start(f32[4,4]{1,0:T(4,128)} %convert_element_type.88) | copy-start | bytes 196
  15.7 1.5 %copy-start.23 = (f32[1,2]{1,0:T(1,128)S(1)}, f32[1,2]{1,0:T(1,128)}, u32[]{:S(2)}) copy-start(f32[1,2]{1,0:T(1,128)} %param.18) | copy-start | bytes 28
  17.2 2.3 %copy-start.6 = (f32[4,2,128,4,128]{2,4,3,1,0:T(8,128)}, f32[4,2,128,4,128]{2,4,3,1,0:T(8,128)S(1)}, u32[]{:S(2)}) copy-start(f32[4,2,128,4,128]{2,4,3,1,0:T(8,128)S(1)} %get-tuple-element.23) | copy-start | bytes 6291460
  17.2 2.3 %copy-start.21 = (f32[4,2,128]{2,1,0:T(2,128)}, f32[4,2,128]{2,1,0:T(2,128)S(1)}, u32[]{:S(2)}) copy-start(f32[4,2,128]{2,1,0:T(2,128)S(1)} %get-tuple-element.22) | copy-start | bytes 12292
  17.2 1.4 %copy-start.5 = (bf16[16,128,2,64]{1,3,2,0:T(8,128)(2,1)S(1)}, bf16[16,128,2,64]{1,3,2,0:T(8,128)(2,1)}, u32[]{:S(2)}) copy-start(bf16[16,128,2,64]{1,3,2,0:T(8,128)(2,1)} %gather_fusion.1) | copy-start | bytes 1572868
  21.9 1.7 %copy-start.20 = (s32[4,4]{1,0:T(4,128)S(1)}, s32[4,4]{1,0:T(4,128)}, u32[]{:S(2)}) copy-start(s32[4,4]{1,0:T(4,128)} %copy-done.19) | copy-start | bytes 196
  26.9 1.6 %copy-start.4 = (bf16[1,3,1024,128]{3,2,1,0:T(8,128)(2,1)S(1)}, bf16[1,3,1024,128]{3,2,1,0:T(8,128)(2,1)}, u32[]{:S(2)}) copy-start(bf16[1,3,1024,128]{3,2,1,0:T(8,128)(2,1)} %param.14) | copy-start | bytes 2359300
  28.6 1.2 copy-start.3
  28.6 1.5 %copy-start.24 = (bf16[1,512,1024]{2,1,0:T(8,128)(2,1)S(1)}, bf16[1,512,1024]{2,1,0:T(8,128)(2,1)}, u32[]{:S(2)}) copy-start(bf16[1,512,1024]{2,1,0:T(8,128)(2,1)} %param.17) | copy-start | bytes 3145732
  28.6 1.8 %copy-start.25 = (f32[512,512]{1,0:T(8,128)S(1)}, f32[512,512]{1,0:T(8,128)}, u32[]{:S(2)}) copy-start(f32[512,512]{1,0:T(8,128)} %fusion.20) | copy-start | bytes 3145732
  31.5 1.8 %copy-start.8 = (bf16[512,512]{1,0:T(8,128)(2,1)}, bf16[512,512]{1,0:T(8,128)(2,1)S(1)}, u32[]{:S(2)}) copy-start(bf16[512,512]{1,0:T(8,128)(2,1)S(1)} %fusion.7) | copy-start | bytes 1572868
  33.2 34.8 %copy-start.13 = (f32[1,1024]{1,0:T(1,128)S(1)}, f32[1,1024]{1,0:T(1,128)}, u32[]{:S(2)}) copy-start(f32[1,1024]{1,0:T(1,128)} %param.13) | copy-start | bytes 12292
  33.2 33.4 %all-to-all-start = ((bf16[8,64,1024]{2,1,0:T(8,128)(2,1)}), bf16[8,64,1024]{2,1,0:T(8,128)(2,1)}, u32[]{:S(2)}, u32[]{:S(2)}) async-start(bf16[8,64,1024]{2,1,0:T(8,128)(2,1)} %bitcast.164), calls=%async_computation | async-start | bytes 2097152 | tf_op jit(solution)/shard_map/all_to_all | solution.py:21
  69.2 26.2 %copy-start.15 = (f32[4,4]{1,0:T(4,128)S(1)}, f32[4,4]{1,0:T(4,128)}, u32[]{:S(2)}) copy-start(f32[4,4]{1,0:T(4,128)} %convert_element_type.88) | copy-start | bytes 196
  69.2 26.2 %copy-start.22 = (f32[4,2,128]{2,1,0:T(2,128)S(1)}, f32[4,2,128]{2,1,0:T(2,128)}, u32[]{:S(2)}) copy-start(f32[4,2,128]{2,1,0:T(2,128)} %copy-done.21) | copy-start | bytes 12292
  70.3 19.1 %collective-permute-start = (bf16[64,1024]{1,0:T(8,128)(2,1)S(1)}, bf16[64,1024]{1,0:T(8,128)(2,1)S(1)}, u32[]{:S(2)}, u32[]{:S(2)}) collective-permute-start(bf16[64,1024]{1,0:T(8,128)(2,1)S(1)} %add_convert_fusion.1), channel_id=1, source_target_pairs={{0,248},{8,0},{16,8},{24,16},{32,24},{40,32},{48,40},{56,48},{64,5... | collective-permute-start | bytes 393224 | tf_op jit(solution)/shard_map/ppermute | solution.py:36
  90.5 30.8 %all-to-all-start.1 = ((bf16[8,64,1024]{2,1,0:T(8,128)(2,1)}), bf16[8,64,1024]{2,1,0:T(8,128)(2,1)}, u32[]{:S(2)}, u32[]{:S(2)}) async-start(bf16[8,64,1024]{2,1,0:T(8,128)(2,1)} %broadcast_in_dim.14), calls=%async_computation.1 | async-start | bytes 2097152 | tf_op jit(solution)/shard_map/all_to_all | solution.py:27
  98.9 2.5 %copy-start.9 = (bf16[512,512]{1,0:T(8,128)(2,1)S(1)}, bf16[512,512]{1,0:T(8,128)(2,1)}, u32[]{:S(2)}) copy-start(bf16[512,512]{1,0:T(8,128)(2,1)} %copy-done.8) | copy-start | bytes 1572868
  100.4 2.7 %copy-start.26 = (f32[512,512]{1,0:T(8,128)S(1)}, f32[512,512]{1,0:T(8,128)}, u32[]{:S(2)}) copy-start(f32[512,512]{1,0:T(8,128)} %fusion.20) | copy-start | bytes 3145732
  103.1 1.7 %copy-start.11 = (f32[8,1,1024]{2,1,0:T(1,128)S(1)}, f32[8,1,1024]{2,1,0:T(1,128)}, u32[]{:S(2)}) copy-start(f32[8,1,1024]{2,1,0:T(1,128)} %all_to_all.16) | copy-start | bytes 98308
where the time goes:
time: 124 us; the launch traced here: 123 us
  waiting for transfers between devices  40.8 us (33%)
  matrix products  24.1 us (19%)
  starting transfers between devices  22.3 us (18%)
  other arithmetic  13.3 us (11%)
  local copies, waits for them, and re-layouts  11.9 us (10%)
  blocking collectives  9.17 us (7%)
  between operations  1.93 us (2%)
    all_to_all x1, waiting for transfers between devices, summed_on_arrival(): lax.all_to_all(in_blocks(value, dim, devices), axis, 0, 0, tiled=True)  25.1 us
    all_to_all x1, waiting for transfers between devices, from_everyone(): return lax.all_to_all(copies, axis, split_axis=0, concat_axis=0, tiled=True)  15.8 us
    ppermute x1, starting transfers between devices, from_behind(): lax.ppermute(value, axis, [(i, (i + by) % devices) for i in range(devices)])  9.87 us
    all_to_all x1, blocking collectives, from_everyone(): return lax.all_to_all(copies, axis, split_axis=0, concat_axis=0, tiled=True)  9.17 us
    all_to_all x1, starting transfers between devices, summed_on_arrival(): lax.all_to_all(in_blocks(value, dim, devices), axis, 0, 0, tiled=True)  7.54 us
    dot_general x6, matrix products, batched_product(): return jnp.einsum(form, left, right, preferred_element_type=jnp.float32)  6.32 us
    all_to_all x1, starting transfers between devices, from_everyone(): return lax.all_to_all(copies, axis, split_axis=0, concat_axis=0, tiled=True)  4.9 us
    unnamed x55, local copies, waits for them, and re-layouts  3.96 us
  transfers between devices with their start and end apart: 3, of which 2 were waited for; matrix products, arithmetic and copies ran while one was open for 9% of the time, Pallas kernels for 0%

commit v1 on v0

v1 whole, which is shorter than its diff:
```python
import functools

import jax
import jax.numpy as jnp
from jax import lax
from jax.experimental import pallas as pl
from jax.experimental.pallas import tpu as pltpu
from jax.sharding import PartitionSpec as P

BLK = 128
ROWS = 32

root_half = 0.7071067811865476
normal_peak = 0.3989422804014327

F32 = jnp.float32
BF16 = jnp.bfloat16


def dot_nn(left, right):
    return lax.dot_general(left, right, (((1,), (0,)), ((), ())), preferred_element_type=F32)


def dot_nt(left, right):
    return lax.dot_general(left, right, (((1,), (1,)), ((), ())), preferred_element_type=F32)


def dot_tn(left, right):
    return lax.dot_general(left, right, (((0,), (0,)), ((), ())), preferred_element_type=F32)


def section_kernel(
    patch_ref,
    near_ref,
    valid_ref,
    scale_ref,
    gain_ref,
    x_hbm,
    g_hbm,
    qkv_hbm,
    out_hbm,
    up_hbm,
    down_hbm,
    part_ref,
    grad_scale_ref,
    grad_qkv_hbm,
    grad_out_hbm,
    grad_up_hbm,
    grad_down_hbm,
    x_v,
    g_v,
    w_v,
    v_v,
    normed,
    raw,
    back,
    q_heads,
    k_all,
    v_all,
    datt_heads,
    cosine,
    d_weight,
    weight_b,
    d_cos,
    left_t,
    mask,
    hidden,
    d_all,
    grad_w,
    grad_v,
    in_sem,
    out_sem,
):
    tokens, width = x_v.shape
    cols = out_hbm.shape[0]
    units = down_hbm.shape[0]
    half = cols // 2
    blocks = tokens // BLK

    loads = [
        pltpu.make_async_copy(x_hbm, x_v, in_sem.at[0]),
        pltpu.make_async_copy(qkv_hbm.at[0, 0], w_v.at[:, pl.ds(0, cols)], in_sem.at[1]),
        pltpu.make_async_copy(qkv_hbm.at[0, 1], w_v.at[:, pl.ds(cols, cols)], in_sem.at[2]),
        pltpu.make_async_copy(qkv_hbm.at[0, 2], w_v.at[:, pl.ds(2 * cols, cols)], in_sem.at[3]),
        pltpu.make_async_copy(g_hbm, g_v, in_sem.at[4]),
        pltpu.make_async_copy(out_hbm, v_v.at[pl.ds(0, cols), :], in_sem.at[5]),
        pltpu.make_async_copy(up_hbm.at[0], w_v.at[:, pl.ds(3 * cols, units)], in_sem.at[6]),
        pltpu.make_async_copy(down_hbm, v_v.at[pl.ds(cols, units), :], in_sem.at[7]),
    ]
    for load in loads:
        load.start()

    patch = patch_ref[0]
    for b in range(blocks):
        for m in range(blocks):
            live = jnp.int32(0)
            for j in range(blocks):
                live = live + jnp.where(near_ref[patch, b, j] == m, valid_ref[patch, b, j], 0)
            mask[b, :, m * BLK : (m + 1) * BLK] = jnp.full((8, BLK), live, jnp.int32).astype(F32)

    loads[0].wait()

    def norm_rows(i, carry):
        at = pl.ds(pl.multiple_of(i * ROWS, ROWS), ROWS)
        value = x_v[at, :].astype(F32)
        centred = value - jnp.mean(value, -1, keepdims=True)
        inv_spread = lax.rsqrt(jnp.mean(centred * centred, -1, keepdims=True) + 1e-05)
        normed[at, :] = (centred * inv_spread * gain_ref[...]).astype(BF16)
        return carry

    lax.fori_loop(0, tokens // ROWS, norm_rows, 0, unroll=2)

    for load in loads[1:6]:
        load.wait()
    raw[:, : 3 * cols] = dot_nn(normed[...], w_v[:, : 3 * cols])
    loads[6].wait()
    raw[:, 3 * cols :] = dot_nn(normed[...], w_v[:, 3 * cols :])
    loads[7].wait()
    back[...] = dot_nt(g_v[...], v_v[...])

    def head_spread(total, first):
        low = lax.rsqrt(jnp.sum(jnp.where(first, total, 0.0), -1, keepdims=True) + 1e-06)
        high = lax.rsqrt(jnp.sum(jnp.where(first, 0.0, total), -1, keepdims=True) + 1e-06)
        return jnp.where(first, low, high)

    def head_sums(total, first):
        low = jnp.sum(jnp.where(first, total, 0.0), -1, keepdims=True)
        high = jnp.sum(jnp.where(first, 0.0, total), -1, keepdims=True)
        return jnp.where(first, low, high)

    for b in range(blocks):
        at = slice(b * BLK, (b + 1) * BLK)
        first = lax.broadcasted_iota(jnp.int32, (BLK, cols), 1) < half
        top = lax.broadcasted_iota(jnp.int32, (cols, BLK), 0) < half
        raw_q = raw[at, :cols]
        unit = raw_q * head_spread(raw_q * raw_q, first)
        d_att = back[at, :cols]
        for member, source, heads in ((0, unit, q_heads), (1, d_att, datt_heads)):
            heads[0, at, :] = jnp.where(first, source, 0.0).astype(BF16)
            heads[1, at, :] = jnp.where(first, 0.0, source).astype(BF16)
            flipped = source.T
            left_t[member, :, b * BLK : (b + 1) * BLK] = jnp.where(top, flipped, 0.0).astype(BF16)
            left_t[member, :, tokens + b * BLK : tokens + (b + 1) * BLK] = jnp.where(
                top, 0.0, flipped
            ).astype(BF16)
        raw_k = raw[at, cols : 2 * cols]
        k_all[at, :] = (raw_k * head_spread(raw_k * raw_k, first)).astype(BF16)
        v_all[at, :] = raw[at, 2 * cols : 3 * cols].astype(BF16)

    for h in range(2):
        cosine[h] = dot_nt(q_heads[h], k_all[...])
        d_weight[h] = dot_nt(datt_heads[h], v_all[...])

    def attend_rows(i, sums):
        at = pl.ds(pl.multiple_of(i * ROWS, ROWS), ROWS)
        live = mask[i // (BLK // ROWS), 0:1, :]
        fresh = []
        for h in range(2):
            factor = scale_ref[0, h]
            cos = cosine[h, at, :]
            exponent = jnp.exp(factor * cos - factor) * live
            weights = exponent * (1.0 / jnp.sum(exponent, -1, keepdims=True))
            d_w = d_weight[h, at, :]
            inner = jnp.sum(weights * d_w, -1, keepdims=True)
            d_score = weights * (d_w - inner)
            spot = pl.ds(pl.multiple_of(h * tokens + i * ROWS, ROWS), ROWS)
            weight_b[spot, :] = weights.astype(BF16)
            d_cos[spot, :] = (d_score * factor).astype(BF16)
            fresh.append(sums[h] + d_score * cos)
        return tuple(fresh)

    def hidden_rows(i):
        at = pl.ds(pl.multiple_of(i * ROWS, ROWS), ROWS)
        pre = raw[at, 3 * cols :]
        cdf = 0.5 * (1.0 + lax.erf(pre * root_half))
        hidden[at, cols:] = (pre * cdf).astype(BF16)
        slope = cdf + pre * jnp.exp(-0.5 * pre * pre) * normal_peak
        d_all[at, 3 * cols :] = (back[at, cols:] * slope).astype(BF16)

    def both_rows(i, sums):
        hidden_rows(i)
        return attend_rows(i, sums)

    zero = jnp.zeros((ROWS, tokens), F32)
    sums = lax.fori_loop(0, tokens // ROWS, both_rows, (zero, zero))
    for h in range(2):
        grad_scale_ref[0, h] = jnp.sum(sums[h])

    first = lax.broadcasted_iota(jnp.int32, (tokens, cols), 1) < half
    hidden[:, :cols] = jnp.where(
        first, dot_nn(weight_b[:tokens, :], v_all[...]), dot_nn(weight_b[tokens:, :], v_all[...])
    ).astype(BF16)
    d_q = jnp.where(
        first, dot_nn(d_cos[:tokens, :], k_all[...]), dot_nn(d_cos[tokens:, :], k_all[...])
    )
    d_k = dot_nn(left_t[0], d_cos[...]).T
    d_all[:, 2 * cols : 3 * cols] = dot_nn(left_t[1], weight_b[...]).T.astype(BF16)
    for i, d_unit in ((0, d_q), (1, d_k)):
        value = raw[:, i * cols : (i + 1) * cols]
        inv = head_spread(value * value, first)
        inner = head_sums(d_unit * value, first)
        d_all[:, i * cols : (i + 1) * cols] = (
            inv * d_unit - inv * inv * inv * inner * value
        ).astype(BF16)

    part_ref[...] = dot_nt(d_all[...], w_v[...]).astype(BF16)

    stores = []
    step = 256
    for start in range(0, width, step):
        at = slice(start, start + step)
        grad_w[at, :] = dot_tn(normed[:, at], d_all[...]).astype(BF16)
    for i in range(3):
        stores.append(
            pltpu.make_async_copy(
                grad_w.at[:, pl.ds(i * cols, cols)], grad_qkv_hbm.at[0, i], out_sem.at[i]
            )
        )
    stores.append(
        pltpu.make_async_copy(grad_w.at[:, pl.ds(3 * cols, units)], grad_up_hbm.at[0], out_sem.at[3])
    )
    for store in stores:
        store.start()
    grad_v[...] = dot_tn(hidden[...], g_v[...]).astype(BF16)
    stores.append(
        pltpu.make_async_copy(grad_v.at[pl.ds(0, cols), :], grad_out_hbm, out_sem.at[4])
    )
    stores.append(
        pltpu.make_async_copy(grad_v.at[pl.ds(cols, units), :], grad_down_hbm, out_sem.at[5])
    )
    for store in stores[4:]:
        store.start()
    for store in stores:
        store.wait()


def section_terms(x, g, gain, qkv, out, up, down, scale, near, valid, patch):
    tokens, width = x.shape
    cols = out.shape[1]
    units = down.shape[1]
    wide = 3 * cols + units
    tall = cols + units
    smem = pl.BlockSpec(memory_space=pltpu.SMEM)
    vmem = pl.BlockSpec(memory_space=pltpu.VMEM)
    hbm = pl.BlockSpec(memory_space=pl.ANY)
    shape = jax.ShapeDtypeStruct
    return pl.pallas_call(
        section_kernel,
        out_shape=(
            shape((tokens, width), BF16),
            shape((1, 2), F32),
            shape(qkv.shape, BF16),
            shape((cols, width), BF16),
            shape(up.shape, BF16),
            shape((units, width), BF16),
        ),
        in_specs=[smem, smem, smem, smem, vmem, hbm, hbm, hbm, hbm, hbm, hbm],
        out_specs=[vmem, smem, hbm, hbm, hbm, hbm],
        scratch_shapes=[
            pltpu.VMEM((tokens, width), BF16),
            pltpu.VMEM((tokens, width), BF16),
            pltpu.VMEM((width, wide), BF16),
            pltpu.VMEM((tall, width), BF16),
            pltpu.VMEM((tokens, width), BF16),
            pltpu.VMEM((tokens, wide), F32),
            pltpu.VMEM((tokens, tall), F32),
            pltpu.VMEM((2, tokens, cols), BF16),
            pltpu.VMEM((tokens, cols), BF16),
            pltpu.VMEM((tokens, cols), BF16),
            pltpu.VMEM((2, tokens, cols), BF16),
            pltpu.VMEM((2, tokens, tokens), F32),
            pltpu.VMEM((2, tokens, tokens), F32),
            pltpu.VMEM((2 * tokens, tokens), BF16),
            pltpu.VMEM((2 * tokens, tokens), BF16),
            pltpu.VMEM((2, cols, 2 * tokens), BF16),
            pltpu.VMEM((tokens // BLK, 8, tokens), F32),
            pltpu.VMEM((tokens, tall), BF16),
            pltpu.VMEM((tokens, wide), BF16),
            pltpu.VMEM((width, wide), BF16),
            pltpu.VMEM((tall, width), BF16),
            pltpu.SemaphoreType.DMA((8,)),
            pltpu.SemaphoreType.DMA((6,)),
        ],
        compiler_params=pltpu.CompilerParams(vmem_limit_bytes=56 * 1024 * 1024),
        name="section_terms",
    )(patch, near, valid, scale, gain, x, g, qkv, out[0], up, down[0])


def in_blocks(value, dim, devices):
    lengths = value.shape
    pieces = value.reshape(*lengths[:dim], devices, lengths[dim] // devices, *lengths[dim + 1 :])
    return jnp.moveaxis(pieces, dim, 0)


def summed_on_arrival(value, axis, dim):
    devices = lax.axis_size(axis)
    pieces = lax.all_to_all(in_blocks(value, dim, devices), axis, 0, 0, tiled=True)
    return jnp.sum(pieces.astype(jnp.float32), axis=0)


def from_everyone(value, axis):
    copies = jnp.broadcast_to(value, (lax.axis_size(axis), *value.shape))
    return lax.all_to_all(copies, axis, split_axis=0, concat_axis=0, tiled=True)


def taken_together(value, axis):
    return from_everyone(value, axis).sum(axis=0)


def from_behind(value, axis, by):
    devices = lax.axis_size(axis)
    return lax.ppermute(value, axis, [(i, (i + by) % devices) for i in range(devices)])


def joined_along(pieces, dim):
    lengths = list(pieces.shape[1:])
    lengths[dim] *= pieces.shape[0]
    return jnp.moveaxis(pieces, 0, dim).reshape(lengths)


def gathered_copies(value, axis, dim):
    return joined_along(from_everyone(value, axis), dim)


def norm_back(d_normed, grad_rows, standard, inv_spread, gain):
    scaled = d_normed * gain
    first_mean = jnp.mean(scaled, -1, keepdims=True)
    second_mean = jnp.mean(scaled * standard, -1, keepdims=True)
    d_input = (
        grad_rows.astype(jnp.float32) + inv_spread * (scaled - first_mean - standard * second_mean)
    ).astype(jnp.bfloat16)
    gain_grad = jnp.sum(d_normed * standard, 0)
    return (d_input, gain_grad)


def shards(x, g, gain, qkv, out, up, down, scale, near, valid, patch):
    part, grad_scale, grad_qkv, grad_out, grad_up, grad_down = section_terms(
        x, g, gain, qkv, out, up, down, scale, near, valid, patch
    )
    row_count = x.shape[0] // lax.axis_size("tp")
    row_start = lax.axis_index("tp") * row_count
    share = summed_on_arrival(part, "tp", 0)
    grad_share = lax.dynamic_slice_in_dim(g, row_start, row_count, 0)
    as_float = lax.dynamic_slice_in_dim(x, row_start, row_count, 0).astype(jnp.float32)
    centred = as_float - jnp.mean(as_float, -1, keepdims=True)
    inv_spread = lax.rsqrt(jnp.mean(centred * centred, -1, keepdims=True) + 1e-05)
    input_share, gain_part = norm_back(share, grad_share, centred * inv_spread, inv_spread, gain[0])
    gain_grad = taken_together(gain_part, "tp")
    shifted = from_behind(input_share, "segment", -1)
    received = gathered_copies(shifted, "tp", 0)
    return (
        received,
        grad_qkv,
        grad_out[None],
        grad_up,
        grad_down[None],
        gain_grad[None],
        grad_scale,
    )


def solution(mesh):
    placed = (
        P("segment", None),
        P("segment", None),
        P("segment", None),
        P("segment", None, None, "tp"),
        P("segment", "tp", None),
        P("segment", None, "tp"),
        P("segment", "tp", None),
        P("segment", "tp"),
        P(),
        P(),
        P("segment"),
    )
    return jax.shard_map(
        shards,
        mesh=mesh,
        in_specs=placed,
        out_specs=(
            P("segment", None),
            P("segment", None, None, "tp"),
            P("segment", "tp", None),
            P("segment", None, "tp"),
            P("segment", "tp", None),
            P("segment", None),
            P("segment", "tp"),
        ),
        check_vma=False,
    )
```

time: 124 us -> 108 us (0.87)
  matrix products: 24.1 us -> 0 us
  Pallas kernels: 0 us -> 19.1 us
  other arithmetic: 13.3 us -> 2.42 us
  waiting for transfers between devices: 40.8 us -> 50.5 us
  local copies, waits for them, and re-layouts: 11.9 us -> 4.92 us
  starting transfers between devices: 22.3 us -> 21 us
    dot_general x24 -> x0, matrix products: 24.1 us -> none  [the longest x6 6.32 us: batched_product(): return jnp.einsum(form, left, right, preferred_element_type=jnp.float32)]
    pallas_call x0 -> x1, Pallas kernels: none -> 19.1 us  [section_terms(): pl.pallas_call(section_kernel, out_shape=(shape((tokens, width), BF16), s...]
    all_to_all x1, waiting for transfers between devices: 15.8 us -> 25.1 us  [from_everyone(): return lax.all_to_all(copies, axis, split_axis=0, concat_axis=0, tiled=True)]
    reduce_sum x6 -> x2, other arithmetic: 4.95 us -> 0.32 us  [the longest x1 0.2 us: shards(): jnp.mean(centred * centred, -1, keepdims=True) + 1e-05]
    gather x2 -> x0, local copies, waits for them, and re-layouts: 2.3 us -> none  [the longest x1 1.53 us: layer_terms(): v_near = values[neighbours]]
    dot_general x3 -> x0, local copies, waits for them, and re-layouts: 2.06 us -> none  [layer_terms(): jnp.dot(unit_scaled, qkv_part[member], preferred_element_type=jnp.float32)]
    mul x3 -> x0, other arithmetic: 1.7 us -> none  [the longest x1 1.68 us: layer_terms(): standard = centred * inv_spread]
    reshape x5 -> x0, local copies, waits for them, and re-layouts: 1.4 us -> none  [the longest x1 1.05 us: layer_terms(): jnp.einsum('bjm,bjthd->mthd', one_hot, key_terms)]
  transfers between devices with their start and end apart: 3 -> 3, of which waited for: 2 -> 2; matrix products, arithmetic and copies ran while one was open for 9% -> 1% of each run, Pallas kernels for 0% -> 0%
where the time goes in v1:
time: 108 us
  waiting for transfers between devices  50.5 us (47%)
  starting transfers between devices  21 us (19%)
  Pallas kernels  19.1 us (18%)
  blocking collectives  8.49 us (8%)
  local copies, waits for them, and re-layouts  4.92 us (5%)
  other arithmetic  2.42 us (2%)
  between operations  1.33 us (1%)
    all_to_all x1, waiting for transfers between devices, summed_on_arrival(): lax.all_to_all(in_blocks(value, dim, devices), axis, 0, 0, tiled=True)  25.4 us
    all_to_all x1, waiting for transfers between devices, from_everyone(): return lax.all_to_all(copies, axis, split_axis=0, concat_axis=0, tiled=True)  25.1 us
    pallas_call x1, Pallas kernels, section_terms(): pl.pallas_call(section_kernel, out_shape=(shape((tokens, width), BF16), s...  19.1 us
    ppermute x1, starting transfers between devices, from_behind(): lax.ppermute(value, axis, [(i, (i + by) % devices) for i in range(devices)])  9.22 us
    all_to_all x1, blocking collectives, from_everyone(): return lax.all_to_all(copies, axis, split_axis=0, concat_axis=0, tiled=True)  8.49 us
    all_to_all x1, starting transfers between devices, summed_on_arrival(): lax.all_to_all(in_blocks(value, dim, devices), axis, 0, 0, tiled=True)  7.54 us
    all_to_all x1, starting transfers between devices, from_everyone(): return lax.all_to_all(copies, axis, split_axis=0, concat_axis=0, tiled=True)  4.24 us
    unnamed x7, local copies, waits for them, and re-layouts  3.81 us
  transfers between devices with their start and end apart: 3, of which 2 were waited for; matrix products, arithmetic and copies ran while one was open for 1% of the time, Pallas kernels for 0%

profile of v1, /device:TPU:1, one launch (start us, length us, event | category | flops | bytes accessed | tf_op | source)
XLA Modules:
  0.0 107.7 jit_solution(16755488745293955526)
XLA Ops:
  1.3 1.4 %copy.22.near_ref = s32[32,4,4]{2,1,0:T(4,128)} copy(s32[32,4,4]{0,2,1:T(4,128)} %param.19) | data formatting | bytes 4096 | tf_op args[8]
  2.7 1.4 %copy.23.valid_ref = s32[32,4,4]{2,1,0:T(4,128)} copy(s32[32,4,4]{0,2,1:T(4,128)} %param.20) | data formatting | bytes 4096 | tf_op args[9]
  4.1 19.1 %section_terms.1 = (bf16[512,1024]{1,0:T(8,128)(2,1)}, f32[1,2]{1,0:T(1,128)}, bf16[1,3,1024,128]{3,2,1,0:T(8,128)(2,1)}, bf16[128,1024]{1,0:T(8,128)(2,1)}, bf1...) custom-call(s32[1]{0:T(128)S(6)} %copy.27.patch_ref, s32[32,4,4]{2,1,0:T(4,128)} %copy.22.near_ref, ...), custom_call_target="tpu_custom_call" | custom-call | tf_op jit(solution)/shard_map/section_terms/pallas_call | solution.py:247
  23.2 0.0 copy-start
  23.2 7.5 %all-to-all-start = ((bf16[8,64,1024]{2,1,0:T(8,128)(2,1)}), bf16[8,64,1024]{2,1,0:T(8,128)(2,1)S(1)}, u32[]{:S(2)}, u32[]{:S(2)}) async-start(bf16[8,64,1024]{2,1,0:T(8,128)(2,1)} %bitcast.10), calls=%async_computation | async-start | bytes 2097152 | tf_op jit(solution)/shard_map/all_to_all | solution.py:297
  30.7 0.0 copy-start.1
  30.7 0.0 copy-done
  30.7 0.1 convert_reduce_fusion.1
  30.9 0.2 fusion.11
  31.1 25.4 %all-to-all-done = bf16[8,64,1024]{2,1,0:T(8,128)(2,1)S(1)} async-done(((bf16[8,64,1024]{2,1,0:T(8,128)(2,1)}), bf16[8,64,1024]{2,1,0:T(8,128)(2,1)S(1)}, u32[]{:S(2)}, u32[]{:S(2)}) %all-to-all-start) | async-done | bytes 1048608 | tf_op jit(solution)/shard_map/all_to_all | solution.py:297
  56.5 0.2 convert_reduce_fusion
  56.6 0.0 copy-done.1
  56.6 0.2 fusion.10
  56.9 1.1 fusion.9
  57.9 9.2 %collective-permute-start = (bf16[64,1024]{1,0:T(8,128)(2,1)S(1)}, bf16[64,1024]{1,0:T(8,128)(2,1)S(1)}, u32[]{:S(2)}, u32[]{:S(2)}) collective-permute-start(bf16[64,1024]{1,0:T(8,128)(2,1)S(1)} %fusion.9), channel_id=1, source_target_pairs={{0,248},{8,0},{16,8},{24,16},{32,24},{40,32},{48,40},{56,48},{64,5... | collective-permute-start | bytes 393224 | tf_op jit(solution)/shard_map/ppermute | solution.py:312
  67.2 8.5 %all_to_all.16 = f32[8,1,1024]{2,1,0:T(1,128)S(1)} all-to-all(f32[8,1,1024]{2,1,0:T(1,128)S(1)} %broadcast_in_dim.22), channel_id=1, replica_groups=mesh['segment'=32,'tp'=8] {'tp'}, dimensions={0} | all-to-all | bytes 65536 | tf_op jit(solution)/shard_map/all_to_all | solution.py:303
  75.7 0.0 collective-permute-done
  75.7 1.1 %broadcast_in_dim.19 = bf16[8,64,1024]{2,1,0:T(8,128)(2,1)} broadcast(bf16[64,1024]{1,0:T(8,128)(2,1)S(1)} %collective-permute-done), dimensions={1,2} | broadcast | bytes 1179648 | tf_op jit(solution)/shard_map/broadcast_in_dim | solution.py:302
  76.8 4.2 %all-to-all-start.1 = ((bf16[8,64,1024]{2,1,0:T(8,128)(2,1)}), bf16[8,64,1024]{2,1,0:T(8,128)(2,1)S(1)}, u32[]{:S(2)}, u32[]{:S(2)}) async-start(bf16[8,64,1024]{2,1,0:T(8,128)(2,1)} %broadcast_in_dim.19), calls=%async_computation.1 | async-start | bytes 2097152 | tf_op jit(solution)/shard_map/all_to_all | solution.py:303
  81.0 0.6 reduce_sum.69
  81.6 25.1 %all-to-all-done.1 = bf16[8,64,1024]{2,1,0:T(8,128)(2,1)S(1)} async-done(((bf16[8,64,1024]{2,1,0:T(8,128)(2,1)}), bf16[8,64,1024]{2,1,0:T(8,128)(2,1)S(1)}, u32[]{:S(2)}, u32[]{:S(2)}) %all-to-all-start.1) | async-done | bytes 1048608 | tf_op jit(solution)/shard_map/all_to_all | solution.py:303
  106.8 1.0 copy.28
  (4 shorter events, 0.0 us)
Async XLA Ops:
  23.2 7.6 %copy-start = (bf16[512,1024]{1,0:T(8,128)(2,1)S(1)}, bf16[512,1024]{1,0:T(8,128)(2,1)}, u32[]{:S(2)}) copy-start(bf16[512,1024]{1,0:T(8,128)(2,1)} %x_hbm.1) | copy-start | bytes 3145732
  23.2 33.3 %all-to-all-start = ((bf16[8,64,1024]{2,1,0:T(8,128)(2,1)}), bf16[8,64,1024]{2,1,0:T(8,128)(2,1)S(1)}, u32[]{:S(2)}, u32[]{:S(2)}) async-start(bf16[8,64,1024]{2,1,0:T(8,128)(2,1)} %bitcast.10), calls=%async_computation | async-start | bytes 2097152 | tf_op jit(solution)/shard_map/all_to_all | solution.py:297
  30.7 25.9 %copy-start.1 = (f32[1,1024]{1,0:T(1,128)S(1)}, f32[1,1024]{1,0:T(1,128)}, u32[]{:S(2)}) copy-start(f32[1,1024]{1,0:T(1,128)} %gain_ref.1) | copy-start | bytes 12292
  57.9 17.7 %collective-permute-start = (bf16[64,1024]{1,0:T(8,128)(2,1)S(1)}, bf16[64,1024]{1,0:T(8,128)(2,1)S(1)}, u32[]{:S(2)}, u32[]{:S(2)}) collective-permute-start(bf16[64,1024]{1,0:T(8,128)(2,1)S(1)} %fusion.9), channel_id=1, source_target_pairs={{0,248},{8,0},{16,8},{24,16},{32,24},{40,32},{48,40},{56,48},{64,5... | collective-permute-start | bytes 393224 | tf_op jit(solution)/shard_map/ppermute | solution.py:312
  76.8 30.0 %all-to-all-start.1 = ((bf16[8,64,1024]{2,1,0:T(8,128)(2,1)}), bf16[8,64,1024]{2,1,0:T(8,128)(2,1)S(1)}, u32[]{:S(2)}, u32[]{:S(2)}) async-start(bf16[8,64,1024]{2,1,0:T(8,128)(2,1)} %broadcast_in_dim.19), calls=%async_computation.1 | async-start | bytes 2097152 | tf_op jit(solution)/shard_map/all_to_all | solution.py:303

commit v2 on v1

--- a/solution.py
+++ b/solution.py
@@ -286,75 +286,387 @@
     )(patch, near, valid, scale, gain, x, g, qkv, out[0], up, down[0])
 
 
-def in_blocks(value, dim, devices):
-    lengths = value.shape
-    pieces = value.reshape(*lengths[:dim], devices, lengths[dim] // devices, *lengths[dim + 1 :])
-    return jnp.moveaxis(pieces, dim, 0)
-
-
-def summed_on_arrival(value, axis, dim):
-    devices = lax.axis_size(axis)
-    pieces = lax.all_to_all(in_blocks(value, dim, devices), axis, 0, 0, tiled=True)
-    return jnp.sum(pieces.astype(jnp.float32), axis=0)
-
-
-def from_everyone(value, axis):
-    copies = jnp.broadcast_to(value, (lax.axis_size(axis), *value.shape))
-    return lax.all_to_all(copies, axis, split_axis=0, concat_axis=0, tiled=True)
-
-
-def taken_together(value, axis):
-    return from_everyone(value, axis).sum(axis=0)
-
-
-def from_behind(value, axis, by):
-    devices = lax.axis_size(axis)
-    return lax.ppermute(value, axis, [(i, (i + by) % devices) for i in range(devices)])
-
-
-def joined_along(pieces, dim):
-    lengths = list(pieces.shape[1:])
-    lengths[dim] *= pieces.shape[0]
-    return jnp.moveaxis(pieces, 0, dim).reshape(lengths)
-
-
-def gathered_copies(value, axis, dim):
-    return joined_along(from_everyone(value, axis), dim)
-
-
-def norm_back(d_normed, grad_rows, standard, inv_spread, gain):
-    scaled = d_normed * gain
-    first_mean = jnp.mean(scaled, -1, keepdims=True)
-    second_mean = jnp.mean(scaled * standard, -1, keepdims=True)
-    d_input = (
-        grad_rows.astype(jnp.float32) + inv_spread * (scaled - first_mean - standard * second_mean)
-    ).astype(jnp.bfloat16)
-    gain_grad = jnp.sum(d_normed * standard, 0)
-    return (d_input, gain_grad)
-
-
-def shards(x, g, gain, qkv, out, up, down, scale, near, valid, patch):
+CHUNK = 16
+LAG = 2
+MESH = pl.DeviceIdType.MESH
+
+
+def relay_kernel(
+    sections,
+    members,
+    part,
+    gain_ref,
+    x_hbm,
+    g_hbm,
+    received,
+    gain_out,
+    pair_buf,
+    line_buf,
+    line_out,
+    d_input,
+    x_q,
+    g_q,
+    standard,
+    spread,
+    landed,
+    gain_sum,
+    gain_buf,
+    load_sem,
+    pair_send,
+    pair_recv,
+    line_send,
+    line_recv,
+    shift_send,
+    ring_send,
+    ring_recv,
+    fan_send,
+    fan_recv,
+    gain_send,
+    gain_recv,
+    out_sem,
+):
+    tokens, width = part.shape
+    quarter = tokens // 4
+    chunks = quarter // CHUNK
+    last = members // 2 - 1
+    segment = lax.axis_index("segment")
+    member = lax.axis_index("tp")
+    chip = member // 2
+    core = member % 2
+    partner = chip * 2 + (1 - core)
+    target = (segment + sections - 1) % sections
+    source = (segment + 1) % sections
+    half = sections // 2
+    turn_out = jnp.where(target // half == segment // half, 0, 1)
+    turn_in = jnp.where(source // half == segment // half, 0, 1)
+    target_chip = jnp.where(turn_out == 1, last - chip, chip)
+    source_chip = jnp.where(turn_in == 1, last - chip, chip)
+    at_target = (target, target_chip * 2 + core)
+    at_source = (source, source_chip * 2 + core)
+
+    barrier = pltpu.get_barrier_semaphore()
+    for other in range(1, members):
+        pl.semaphore_signal(
+            barrier, 1, device_id=(segment, (member + other) % members), device_id_type=MESH
+        )
+    pl.semaphore_signal(barrier, 1, device_id=at_target, device_id_type=MESH)
+    pl.semaphore_signal(barrier, 1, device_id=at_source, device_id_type=MESH)
+
+    is_end = jnp.logical_or(chip == 0, chip == last)
+    owned = core * 2 + jnp.where(chip == last, 1, 0)
+    mine = pl.ds(pl.multiple_of(owned * quarter, quarter), quarter)
+    x_load = pltpu.make_async_copy(x_hbm.at[mine, :], x_q, load_sem.at[0])
+    g_load = pltpu.make_async_copy(g_hbm.at[mine, :], g_q, load_sem.at[1])
+
+    @pl.when(is_end)
+    def _():
+        x_load.start()
+        g_load.start()
+
+    pl.semaphore_wait(barrier, members + 1)
+
+    def rows_of(block, piece):
+        return pl.ds(pl.multiple_of(block * quarter + piece * CHUNK, CHUNK), CHUNK)
+
+    def piece_of(piece):
+        return pl.ds(pl.multiple_of(piece * CHUNK, CHUNK), CHUNK)
+
+    def pair_copy(way, piece):
+        return pltpu.make_async_remote_copy(
+            src_ref=part.at[rows_of((1 - core) * 2 + way, piece), :],
+            dst_ref=pair_buf.at[way, piece_of(piece), :],
+            send_sem=pair_send.at[way, piece],
+            recv_sem=pair_recv.at[way, piece],
+            device_id=(segment, partner),
+            device_id_type=MESH,
+        )
+
+    def place(way):
+        return chip if way == 1 else last - chip
+
+    def beyond(way):
+        ahead = jnp.minimum(chip + 1, last) if way == 1 else jnp.maximum(chip - 1, 0)
+        return (segment, ahead * 2 + core)
+
+    def line_copy(way, piece):
+        return pltpu.make_async_remote_copy(
+            src_ref=line_out.at[way, piece_of(piece), :],
+            dst_ref=line_buf.at[way, piece_of(piece), :],
+            send_sem=line_send.at[way, piece],
+            recv_sem=line_recv.at[way, piece],
+            device_id=beyond(way),
+            device_id_type=MESH,
+        )
+
+    def shift_copy(way, piece):
+        entry = jnp.where(turn_out == 1, way, 1 - way)
+        return pltpu.make_async_remote_copy(
+            src_ref=d_input.at[piece_of(piece), :],
+            dst_ref=landed.at[rows_of(core * 2 + way, piece), :],
+            send_sem=shift_send.at[piece],
+            recv_sem=ring_recv.at[entry, piece],
+            device_id=at_target,
+            device_id_type=MESH,
+        )
+
+    def ring_block(way):
+        return jnp.where(turn_in == 1, way, 1 - way)
+
+    def ring_copy(way, piece):
+        rows = landed.at[rows_of(core * 2 + ring_block(way), piece), :]
+        return pltpu.make_async_remote_copy(
+            src_ref=rows,
+            dst_ref=rows,
+            send_sem=ring_send.at[way, piece],
+            recv_sem=ring_recv.at[way, piece],
+            device_id=beyond(way),
+            device_id_type=MESH,
+        )
+
+    def fan_copy(way, piece):
+        rows = landed.at[rows_of(core * 2 + ring_block(way), piece), :]
+        return pltpu.make_async_remote_copy(
+            src_ref=rows,
+            dst_ref=rows,
+            send_sem=fan_send.at[way, piece],
+            recv_sem=fan_recv.at[way, piece],
+            device_id=(segment, partner),
+            device_id_type=MESH,
+        )
+
+    def fan_arrival(way, piece):
+        rows = landed.at[rows_of((1 - core) * 2 + ring_block(way), piece), :]
+        return pltpu.make_async_remote_copy(
+            src_ref=rows,
+            dst_ref=rows,
+            send_sem=fan_send.at[way, piece],
+            recv_sem=fan_recv.at[way, piece],
+            device_id=(segment, partner),
+            device_id_type=MESH,
+        )
+
+    def out_copy(side, way, piece):
+        owner = core if side == 0 else 1 - core
+        rows = rows_of(owner * 2 + ring_block(way), piece)
+        return pltpu.make_async_copy(
+            landed.at[rows, :], received.at[rows, :], out_sem.at[side, way, piece]
+        )
+
+    def gain_copy(slot, other):
+        return pltpu.make_async_remote_copy(
+            src_ref=gain_sum,
+            dst_ref=gain_buf.at[slot],
+            send_sem=gain_send.at[other - 1],
+            recv_sem=gain_recv.at[slot],
+            device_id=(segment, (member + other) % members),
+            device_id_type=MESH,
+        )
+
+    def start_pairs(piece, carry):
+        for way in range(2):
+            pair_copy(way, piece).start()
+        return carry
+
+    lax.fori_loop(0, chunks, start_pairs, 0)
+
+    @pl.when(is_end)
+    def _():
+        x_load.wait()
+        g_load.wait()
+        gain_sum[...] = jnp.zeros_like(gain_sum)
+
+        def norm_rows(i, carry):
+            at = piece_of(i)
+            value = x_q[at, :].astype(F32)
+            centred = value - jnp.mean(value, -1, keepdims=True)
+            inv = lax.rsqrt(jnp.mean(centred * centred, -1, keepdims=True) + 1e-05)
+            standard[at, :] = centred * inv
+            spread[at, :] = jnp.broadcast_to(inv, (CHUNK, 128))
+            return carry
+
+        lax.fori_loop(0, chunks, norm_rows, 0)
+
+    def reduce_step(way, piece):
+        spot = place(way)
+        at = piece_of(piece)
+        pair_copy(way, piece).wait_recv()
+        total = (
+            part[rows_of(core * 2 + way, piece), :].astype(F32)
+            + pair_buf[way, at, :].astype(F32)
+        )
+
+        @pl.when(spot == 0)
+        def _():
+            line_out[way, at, :] = total.astype(BF16)
+            line_copy(way, piece).start()
+
+        @pl.when(jnp.logical_and(spot > 0, spot < last))
+        def _():
+            line_copy(way, piece).wait_recv()
+            line_out[way, at, :] = (total + line_buf[way, at, :].astype(F32)).astype(BF16)
+            line_copy(way, piece).start()
+
+        @pl.when(spot == last)
+        def _():
+            line_copy(way, piece).wait_recv()
+            d_normed = total + line_buf[way, at, :].astype(F32)
+            unit = standard[at, :]
+            scaled = d_normed * gain_ref[...]
+            first_mean = jnp.mean(scaled, -1, keepdims=True)
+            second_mean = jnp.mean(scaled * unit, -1, keepdims=True)
+            inv = spread[at, :][:, :1]
+            d_input[at, :] = (
+                g_q[at, :].astype(F32) + inv * (scaled - first_mean - unit * second_mean)
+            ).astype(BF16)
+            shift_copy(way, piece).start()
+            gain_sum[...] += jnp.sum(d_normed * unit, 0, keepdims=True)
+
+            @pl.when(piece == chunks - 1)
+            def _():
+                slot = jnp.where(chip == last, 2, 0) + core
+                for other in range(1, members):
+                    gain_copy(slot, other).start()
+
+    def gather_step(way, piece):
+        ring_copy(way, piece).wait_recv()
+
+        @pl.when(place(way) < last)
+        def _():
+            ring_copy(way, piece).start()
+
+        fan_copy(way, piece).start()
+        out_copy(0, way, piece).start()
+
+    steps = chunks + LAG * (2 * last + 1)
+
+    def slot(k, carry):
+        for way in range(2):
+            piece = k - LAG * place(way)
+
+            @pl.when(jnp.logical_and(piece >= 0, piece < chunks))
+            def _():
+                reduce_step(way, piece)
+
+        for way in range(2):
+            piece = k - LAG * (last + 1 + place(way))
+
+            @pl.when(jnp.logical_and(piece >= 0, piece < chunks))
+            def _():
+                gather_step(way, piece)
+
+        return carry
+
+    lax.fori_loop(0, steps, slot, 0)
+
+    def finish(piece, carry):
+        for way in range(2):
+            fan_arrival(way, piece).wait_recv()
+            out_copy(1, way, piece).start()
+        return carry
+
+    lax.fori_loop(0, chunks, finish, 0)
+
+    owners = (0, 1, members - 2, members - 1)
+    total = jnp.zeros_like(gain_sum[...])
+    for slot_index, owner in enumerate(owners):
+
+        @pl.when(member != owner)
+        def _():
+            gain_copy(slot_index, 1).wait_recv()
+
+        @pl.when(member == owner)
+        def _():
+            gain_buf[slot_index] = gain_sum[...]
+
+        total = total + gain_buf[slot_index]
+    gain_out[...] = total
+
+    def settle(piece, carry):
+        for way in range(2):
+            pair_copy(way, piece).wait_send()
+            fan_copy(way, piece).wait_send()
+            out_copy(0, way, piece).wait()
+            out_copy(1, way, piece).wait()
+
+            @pl.when(place(way) < last)
+            def _():
+                line_copy(way, piece).wait_send()
+                ring_copy(way, piece).wait_send()
+
+            @pl.when(place(way) == last)
+            def _():
+                shift_copy(way, piece).wait_send()
+
+        return carry
+
+    lax.fori_loop(0, chunks, settle, 0)
+
+    @pl.when(is_end)
+    def _():
+        for other in range(1, members):
+            gain_copy(0, other).wait_send()
+
+
+def relayed(sections, members, part, x, g, gain):
+    tokens, width = x.shape
+    quarter = tokens // 4
+    chunks = quarter // CHUNK
+    vmem = pl.BlockSpec(memory_space=pltpu.VMEM)
+    hbm = pl.BlockSpec(memory_space=pl.ANY)
+    dma = pltpu.SemaphoreType.DMA
+    return pl.pallas_call(
+        functools.partial(relay_kernel, sections, members),
+        out_shape=(
+            jax.ShapeDtypeStruct((tokens, width), BF16),
+            jax.ShapeDtypeStruct((1, width), F32),
+        ),
+        in_specs=[vmem, vmem, hbm, hbm],
+        out_specs=[hbm, vmem],
+        scratch_shapes=[
+            pltpu.VMEM((2, quarter, width), BF16),
+            pltpu.VMEM((2, quarter, width), BF16),
+            pltpu.VMEM((2, quarter, width), BF16),
+            pltpu.VMEM((quarter, width), BF16),
+            pltpu.VMEM((quarter, width), BF16),
+            pltpu.VMEM((quarter, width), BF16),
+            pltpu.VMEM((quarter, width), F32),
+            pltpu.VMEM((quarter, 128), F32),
+            pltpu.VMEM((tokens, width), BF16),
+            pltpu.VMEM((1, width), F32),
+            pltpu.VMEM((4, 1, width), F32),
+            dma((2,)),
+            dma((2, chunks)),
+            dma((2, chunks)),
+            dma((2, chunks)),
+            dma((2, chunks)),
+            dma((chunks,)),
+            dma((2, chunks)),
+            dma((2, chunks)),
+            dma((2, chunks)),
+            dma((2, chunks)),
+            dma((members - 1,)),
+            dma((4,)),
+            dma((2, 2, chunks)),
+        ],
+        compiler_params=pltpu.CompilerParams(
+            collective_id=0, has_side_effects=True, vmem_limit_bytes=32 * 1024 * 1024
+        ),
+        name="relayed",
+    )(part, gain, x, g)
+
+
+def shards(sections, members, x, g, gain, qkv, out, up, down, scale, near, valid, patch):
     part, grad_scale, grad_qkv, grad_out, grad_up, grad_down = section_terms(
         x, g, gain, qkv, out, up, down, scale, near, valid, patch
     )
-    row_count = x.shape[0] // lax.axis_size("tp")
-    row_start = lax.axis_index("tp") * row_count
-    share = summed_on_arrival(part, "tp", 0)
-    grad_share = lax.dynamic_slice_in_dim(g, row_start, row_count, 0)
-    as_float = lax.dynamic_slice_in_dim(x, row_start, row_count, 0).astype(jnp.float32)
-    centred = as_float - jnp.mean(as_float, -1, keepdims=True)
-    inv_spread = lax.rsqrt(jnp.mean(centred * centred, -1, keepdims=True) + 1e-05)
-    input_share, gain_part = norm_back(share, grad_share, centred * inv_spread, inv_spread, gain[0])
-    gain_grad = taken_together(gain_part, "tp")
-    shifted = from_behind(input_share, "segment", -1)
-    received = gathered_copies(shifted, "tp", 0)
+    received, gain_grad = relayed(sections, members, part, x, g, gain)
     return (
         received,
         grad_qkv,
         grad_out[None],
         grad_up,
         grad_down[None],
-        gain_grad[None],
+        gain_grad,
         grad_scale,
     )
 
@@ -374,7 +686,7 @@
         P("segment"),
     )
     return jax.shard_map(
-        shards,
+        functools.partial(shards, mesh.shape["segment"], mesh.shape["tp"]),
         mesh=mesh,
         in_specs=placed,
         out_specs=(

time: 108 us -> 72 us (0.67)
  waiting for transfers between devices: 50.5 us -> 0 us
  Pallas kernels: 19.1 us -> 64.8 us
  starting transfers between devices: 21 us -> 0 us
  blocking collectives: 8.49 us -> 0 us
  other arithmetic: 2.42 us -> 0 us
    all_to_all x2 -> x0, waiting for transfers between devices: 50.5 us -> none  [the longest x1 25.4 us: summed_on_arrival(): lax.all_to_all(in_blocks(value, dim, devices), axis, 0, 0, tiled=True)]
    pallas_call x0 -> x1, Pallas kernels: none -> 45.6 us  [relayed(): pl.pallas_call(functools.partial(relay_kernel, sections, members), out_sh...]
    all_to_all x2 -> x0, starting transfers between devices: 11.8 us -> none  [the longest x1 7.54 us: summed_on_arrival(): lax.all_to_all(in_blocks(value, dim, devices), axis, 0, 0, tiled=True)]
    ppermute x1 -> x0, starting transfers between devices: 9.22 us -> none  [from_behind(): lax.ppermute(value, axis, [(i, (i + by) % devices) for i in range(devices)])]
    all_to_all x1 -> x0, blocking collectives: 8.49 us -> none  [from_everyone(): return lax.all_to_all(copies, axis, split_axis=0, concat_axis=0, tiled=True)]
    unnamed x7 -> x14, local copies, waits for them, and re-layouts: 3.81 us -> 5.63 us
    reduce_sum x5 -> x0, other arithmetic: 1.34 us -> none  [the longest x1 0.62 us: taken_together(): return from_everyone(value, axis).sum(axis=0)]
    broadcast_in_dim x2 -> x0, local copies, waits for them, and re-layouts: 1.12 us -> none  [from_everyone(): copies = jnp.broadcast_to(value, (lax.axis_size(axis), *value.shape))]
  transfers between devices with their start and end apart: 3 -> 0, of which waited for: 2 -> 0; matrix products, arithmetic and copies ran while one was open for 1% -> 0% of each run, Pallas kernels for 0% -> 0%
where the time goes in v2:
time: 72 us; the launch traced here: 71.8 us
  Pallas kernels  64.8 us (90%)
  local copies, waits for them, and re-layouts  5.63 us (8%)
  between operations  1.33 us (2%)
    pallas_call x1, Pallas kernels, relayed(): pl.pallas_call(functools.partial(relay_kernel, sections, members), out_sh...  45.6 us
    pallas_call x1, Pallas kernels, section_terms(): pl.pallas_call(section_kernel, out_shape=(shape((tokens, width), BF16), s...  19.2 us
    unnamed x14, local copies, waits for them, and re-layouts  5.63 us

profile of v2, /device:TPU:1, one launch (start us, length us, event | category | flops | bytes accessed | tf_op | source)
XLA Modules:
  0.0 71.8 jit_solution(4645857889391070813)
XLA Ops:
  1.3 0.0 copy-start.4
  1.3 1.4 %copy.18.near_ref = s32[32,4,4]{2,1,0:T(4,128)} copy(s32[32,4,4]{0,2,1:T(4,128)} %param.19) | data formatting | bytes 4096 | tf_op args[8]
  2.7 0.0 copy-done.4
  2.7 0.7 %copy.19.valid_ref = s32[32,4,4]{2,1,0:T(4,128)} copy(s32[32,4,4]{0,2,1:T(4,128)S(1)} %copy-done.4) | data formatting | bytes 4096 | tf_op args[9]
  3.5 0.0 copy-start
  3.5 0.0 copy-start.1
  3.5 19.2 %section_terms.1 = (bf16[512,1024]{1,0:T(8,128)(2,1)}, f32[1,2]{1,0:T(1,128)}, bf16[1,3,1024,128]{3,2,1,0:T(8,128)(2,1)}, bf16[128,1024]{1,0:T(8,128)(2,1)}, bf1...) custom-call(s32[1]{0:T(128)S(6)} %copy.22.patch_ref, s32[32,4,4]{2,1,0:T(4,128)} %copy.18.near_ref, ...), custom_call_target="tpu_custom_call" | custom-call | tf_op jit(solution)/shard_map/section_terms/pallas_call | solution.py:247
  22.7 0.0 copy-start.3
  22.7 0.0 copy-done
  22.7 0.0 copy-done.1
  22.7 0.7 copy-done.3
  23.3 0.0 copy-start.2
  23.4 1.2 %copy-done.2 = bf16[512,1024]{1,0:T(8,128)(2,1)S(1)} copy-done((bf16[512,1024]{1,0:T(8,128)(2,1)S(1)}, bf16[512,1024]{1,0:T(8,128)(2,1)}, u32[]{:S(2)}) %copy-start.2) | copy-done | bytes 1048600
  24.6 45.6 %relayed.1 = (bf16[512,1024]{1,0:T(8,128)(2,1)S(1)}, f32[1,1024]{1,0:T(1,128)S(1)}) custom-call(bf16[512,1024]{1,0:T(8,128)(2,1)S(1)} %copy-done.2, f32[1,1024]{1,0:T(1,128)S(1)} %copy-done.3, bf16[512,1024]{1,0:T(8,128)(2,1)S(1)} %copy-done, bf16[512,1024]{1,0:T(8,128)(2,1)S(1)} %copy-done.1), custom_call_target="tpu_custom_call" | custom-call | tf_op jit(solution)/shard_map/relayed/pallas_call | solution.py:617
  70.2 1.0 %copy.23 = bf16[512,1024]{1,0:T(8,128)(2,1)} copy(bf16[512,1024]{1,0:T(8,128)(2,1)S(1)} %get-tuple-element.30) | data formatting | bytes 2097152
  71.2 0.6 copy.24
Async XLA Ops:
  1.3 1.4 %copy-start.4 = (s32[32,4,4]{0,2,1:T(4,128)S(1)}, s32[32,4,4]{0,2,1:T(4,128)}, u32[]{:S(2)}) copy-start(s32[32,4,4]{0,2,1:T(4,128)} %param.20) | copy-start | bytes 6148
  3.5 19.2 %copy-start = (bf16[512,1024]{1,0:T(8,128)(2,1)S(1)}, bf16[512,1024]{1,0:T(8,128)(2,1)}, u32[]{:S(2)}) copy-start(bf16[512,1024]{1,0:T(8,128)(2,1)} %x_hbm.3) | copy-start | bytes 3145732
  3.5 19.2 %copy-start.1 = (bf16[512,1024]{1,0:T(8,128)(2,1)S(1)}, bf16[512,1024]{1,0:T(8,128)(2,1)}, u32[]{:S(2)}) copy-start(bf16[512,1024]{1,0:T(8,128)(2,1)} %g_hbm.3) | copy-start | bytes 3145732
  22.7 0.7 copy-start.3
  23.3 1.2 %copy-start.2 = (bf16[512,1024]{1,0:T(8,128)(2,1)S(1)}, bf16[512,1024]{1,0:T(8,128)(2,1)}, u32[]{:S(2)}) copy-start(bf16[512,1024]{1,0:T(8,128)(2,1)} %get-tuple-element.15.part) | copy-start | bytes 3145732

commit v3 on v2

v3 whole, which is shorter than its diff:
```python
import functools

import jax
import jax.numpy as jnp
from jax import lax
from jax.experimental import pallas as pl
from jax.experimental.pallas import tpu as pltpu
from jax.sharding import PartitionSpec as P

BLK = 128
ROWS = 32

root_half = 0.7071067811865476
normal_peak = 0.3989422804014327

F32 = jnp.float32
BF16 = jnp.bfloat16


def dot_nn(left, right):
    return lax.dot_general(left, right, (((1,), (0,)), ((), ())), preferred_element_type=F32)


def dot_nt(left, right):
    return lax.dot_general(left, right, (((1,), (1,)), ((), ())), preferred_element_type=F32)


def dot_tn(left, right):
    return lax.dot_general(left, right, (((0,), (0,)), ((), ())), preferred_element_type=F32)


CHUNK = 16
LAG = 4
GRAD_AT_END = 8
GRAD_AT_MIDDLE = 0
MESH = pl.DeviceIdType.MESH


def section_kernel(
    sections,
    members,
    patch_ref,
    near_ref,
    valid_ref,
    scale_ref,
    gain_ref,
    x_hbm,
    g_hbm,
    qkv_hbm,
    out_hbm,
    up_hbm,
    down_hbm,
    received,
    gain_out,
    grad_scale_ref,
    grad_qkv,
    grad_out,
    grad_up,
    grad_down,
    x_v,
    g_v,
    w_v,
    v_v,
    normed,
    raw,
    back,
    q_heads,
    k_all,
    v_all,
    datt_heads,
    cosine,
    d_weight,
    weight_b,
    d_cos,
    left_t,
    mask,
    hidden,
    d_all,
    part,
    pair_buf,
    line_buf,
    line_out,
    d_input,
    standard,
    spread,
    landed,
    gain_sum,
    gain_buf,
    in_sem,
    pair_send,
    pair_recv,
    line_send,
    line_recv,
    shift_send,
    ring_send,
    ring_recv,
    fan_send,
    fan_recv,
    gain_send,
    gain_recv,
    out_sem,
):
    tokens, width = x_v.shape
    cols = out_hbm.shape[0]
    units = down_hbm.shape[0]
    head = cols // 2
    blocks = tokens // BLK

    quarter = tokens // 4
    chunks = quarter // CHUNK
    last = members // 2 - 1
    segment = lax.axis_index("segment")
    member = lax.axis_index("tp")
    chip = member // 2
    core = member % 2
    partner = chip * 2 + (1 - core)
    target = (segment + sections - 1) % sections
    source = (segment + 1) % sections
    half = sections // 2
    turn_out = jnp.where(target // half == segment // half, 0, 1)
    turn_in = jnp.where(source // half == segment // half, 0, 1)
    target_chip = jnp.where(turn_out == 1, last - chip, chip)
    source_chip = jnp.where(turn_in == 1, last - chip, chip)
    at_target = (target, target_chip * 2 + core)
    at_source = (source, source_chip * 2 + core)

    barrier = pltpu.get_barrier_semaphore()
    for other in range(1, members):
        pl.semaphore_signal(
            barrier, 1, device_id=(segment, (member + other) % members), device_id_type=MESH
        )
    pl.semaphore_signal(barrier, 1, device_id=at_target, device_id_type=MESH)
    pl.semaphore_signal(barrier, 1, device_id=at_source, device_id_type=MESH)

    loads = [
        pltpu.make_async_copy(x_hbm, x_v, in_sem.at[0]),
        pltpu.make_async_copy(qkv_hbm.at[0, 0], w_v.at[:, pl.ds(0, cols)], in_sem.at[1]),
        pltpu.make_async_copy(qkv_hbm.at[0, 1], w_v.at[:, pl.ds(cols, cols)], in_sem.at[2]),
        pltpu.make_async_copy(qkv_hbm.at[0, 2], w_v.at[:, pl.ds(2 * cols, cols)], in_sem.at[3]),
        pltpu.make_async_copy(g_hbm, g_v, in_sem.at[4]),
        pltpu.make_async_copy(out_hbm, v_v.at[pl.ds(0, cols), :], in_sem.at[5]),
        pltpu.make_async_copy(up_hbm.at[0], w_v.at[:, pl.ds(3 * cols, units)], in_sem.at[6]),
        pltpu.make_async_copy(down_hbm, v_v.at[pl.ds(cols, units), :], in_sem.at[7]),
    ]
    for load in loads:
        load.start()

    patch = patch_ref[0]
    for b in range(blocks):
        for m in range(blocks):
            live = jnp.int32(0)
            for j in range(blocks):
                live = live + jnp.where(near_ref[b, j, patch] == m, valid_ref[b, j, patch], 0)
            mask[b, :, m * BLK : (m + 1) * BLK] = jnp.full((8, BLK), live, jnp.int32).astype(F32)

    loads[0].wait()

    def norm_rows(i, carry):
        at = pl.ds(pl.multiple_of(i * ROWS, ROWS), ROWS)
        value = x_v[at, :].astype(F32)
        centred = value - jnp.mean(value, -1, keepdims=True)
        inv_spread = lax.rsqrt(jnp.mean(centred * centred, -1, keepdims=True) + 1e-05)
        normed[at, :] = (centred * inv_spread * gain_ref[...]).astype(BF16)
        return carry

    lax.fori_loop(0, tokens // ROWS, norm_rows, 0, unroll=2)

    for load in loads[1:6]:
        load.wait()
    raw[:, : 3 * cols] = dot_nn(normed[...], w_v[:, : 3 * cols])
    loads[6].wait()
    raw[:, 3 * cols :] = dot_nn(normed[...], w_v[:, 3 * cols :])
    loads[7].wait()
    back[...] = dot_nt(g_v[...], v_v[...])

    def head_spread(total, first):
        low = lax.rsqrt(jnp.sum(jnp.where(first, total, 0.0), -1, keepdims=True) + 1e-06)
        high = lax.rsqrt(jnp.sum(jnp.where(first, 0.0, total), -1, keepdims=True) + 1e-06)
        return jnp.where(first, low, high)

    def head_sums(total, first):
        low = jnp.sum(jnp.where(first, total, 0.0), -1, keepdims=True)
        high = jnp.sum(jnp.where(first, 0.0, total), -1, keepdims=True)
        return jnp.where(first, low, high)

    for b in range(blocks):
        at = slice(b * BLK, (b + 1) * BLK)
        first = lax.broadcasted_iota(jnp.int32, (BLK, cols), 1) < head
        top = lax.broadcasted_iota(jnp.int32, (cols, BLK), 0) < head
        raw_q = raw[at, :cols]
        unit = raw_q * head_spread(raw_q * raw_q, first)
        d_att = back[at, :cols]
        for turn, spread_in, heads in ((0, unit, q_heads), (1, d_att, datt_heads)):
            heads[0, at, :] = jnp.where(first, spread_in, 0.0).astype(BF16)
            heads[1, at, :] = jnp.where(first, 0.0, spread_in).astype(BF16)
            flipped = spread_in.T
            left_t[turn, :, b * BLK : (b + 1) * BLK] = jnp.where(top, flipped, 0.0).astype(BF16)
            left_t[turn, :, tokens + b * BLK : tokens + (b + 1) * BLK] = jnp.where(
                top, 0.0, flipped
            ).astype(BF16)
        raw_k = raw[at, cols : 2 * cols]
        k_all[at, :] = (raw_k * head_spread(raw_k * raw_k, first)).astype(BF16)
        v_all[at, :] = raw[at, 2 * cols : 3 * cols].astype(BF16)

    for h in range(2):
        cosine[h] = dot_nt(q_heads[h], k_all[...])
        d_weight[h] = dot_nt(datt_heads[h], v_all[...])

    def attend_rows(i, sums):
        at = pl.ds(pl.multiple_of(i * ROWS, ROWS), ROWS)
        live = mask[i // (BLK // ROWS), 0:1, :]
        fresh = []
        for h in range(2):
            factor = scale_ref[0, h]
            cos = cosine[h, at, :]
            exponent = jnp.exp(factor * cos - factor) * live
            weights = exponent * (1.0 / jnp.sum(exponent, -1, keepdims=True))
            d_w = d_weight[h, at, :]
            inner = jnp.sum(weights * d_w, -1, keepdims=True)
            d_score = weights * (d_w - inner)
            spot = pl.ds(pl.multiple_of(h * tokens + i * ROWS, ROWS), ROWS)
            weight_b[spot, :] = weights.astype(BF16)
            d_cos[spot, :] = (d_score * factor).astype(BF16)
            fresh.append(sums[h] + d_score * cos)
        return tuple(fresh)

    def hidden_rows(i):
        at = pl.ds(pl.multiple_of(i * ROWS, ROWS), ROWS)
        pre = raw[at, 3 * cols :]
        cdf = 0.5 * (1.0 + lax.erf(pre * root_half))
        hidden[at, cols:] = (pre * cdf).astype(BF16)
        slope = cdf + pre * jnp.exp(-0.5 * pre * pre) * normal_peak
        d_all[at, 3 * cols :] = (back[at, cols:] * slope).astype(BF16)

    def both_rows(i, sums):
        hidden_rows(i)
        return attend_rows(i, sums)

    zero = jnp.zeros((ROWS, tokens), F32)
    sums = lax.fori_loop(0, tokens // ROWS, both_rows, (zero, zero))
    for h in range(2):
        grad_scale_ref[0, h] = jnp.sum(sums[h])

    first = lax.broadcasted_iota(jnp.int32, (tokens, cols), 1) < head
    hidden[:, :cols] = jnp.where(
        first, dot_nn(weight_b[:tokens, :], v_all[...]), dot_nn(weight_b[tokens:, :], v_all[...])
    ).astype(BF16)
    d_q = jnp.where(
        first, dot_nn(d_cos[:tokens, :], k_all[...]), dot_nn(d_cos[tokens:, :], k_all[...])
    )
    d_k = dot_nn(left_t[0], d_cos[...]).T
    d_all[:, 2 * cols : 3 * cols] = dot_nn(left_t[1], weight_b[...]).T.astype(BF16)
    for i, d_unit in ((0, d_q), (1, d_k)):
        value = raw[:, i * cols : (i + 1) * cols]
        inv = head_spread(value * value, first)
        inner = head_sums(d_unit * value, first)
        d_all[:, i * cols : (i + 1) * cols] = (
            inv * d_unit - inv * inv * inv * inner * value
        ).astype(BF16)

    is_end = jnp.logical_or(chip == 0, chip == last)
    owned = core * 2 + jnp.where(chip == last, 1, 0)

    def rows_of(block, piece):
        return pl.ds(pl.multiple_of(block * quarter + piece * CHUNK, CHUNK), CHUNK)

    def piece_of(piece):
        return pl.ds(pl.multiple_of(piece * CHUNK, CHUNK), CHUNK)

    def pair_copy(way, piece):
        return pltpu.make_async_remote_copy(
            src_ref=part.at[rows_of((1 - core) * 2 + way, piece), :],
            dst_ref=pair_buf.at[way, piece_of(piece), :],
            send_sem=pair_send.at[way, piece],
            recv_sem=pair_recv.at[way, piece],
            device_id=(segment, partner),
            device_id_type=MESH,
        )

    def place(way):
        return chip if way == 1 else last - chip

    def beyond(way):
        ahead = jnp.minimum(chip + 1, last) if way == 1 else jnp.maximum(chip - 1, 0)
        return (segment, ahead * 2 + core)

    def line_copy(way, piece):
        return pltpu.make_async_remote_copy(
            src_ref=line_out.at[way, piece_of(piece), :],
            dst_ref=line_buf.at[way, piece_of(piece), :],
            send_sem=line_send.at[way, piece],
            recv_sem=line_recv.at[way, piece],
            device_id=beyond(way),
            device_id_type=MESH,
        )

    def shift_copy(way, piece):
        entry = jnp.where(turn_out == 1, way, 1 - way)
        return pltpu.make_async_remote_copy(
            src_ref=d_input.at[piece_of(piece), :],
            dst_ref=landed.at[rows_of(core * 2 + way, piece), :],
            send_sem=shift_send.at[piece],
            recv_sem=ring_recv.at[entry, piece],
            device_id=at_target,
            device_id_type=MESH,
        )

    def ring_block(way):
        return jnp.where(turn_in == 1, way, 1 - way)

    def ring_copy(way, piece):
        rows = landed.at[rows_of(core * 2 + ring_block(way), piece), :]
        return pltpu.make_async_remote_copy(
            src_ref=rows,
            dst_ref=rows,
            send_sem=ring_send.at[way, piece],
            recv_sem=ring_recv.at[way, piece],
            device_id=beyond(way),
            device_id_type=MESH,
        )

    def fan_copy(way, piece):
        rows = landed.at[rows_of(core * 2 + ring_block(way), piece), :]
        return pltpu.make_async_remote_copy(
            src_ref=rows,
            dst_ref=rows,
            send_sem=fan_send.at[way, piece],
            recv_sem=fan_recv.at[way, piece],
            device_id=(segment, partner),
            device_id_type=MESH,
        )

    def fan_arrival(way, piece):
        rows = landed.at[rows_of((1 - core) * 2 + ring_block(way), piece), :]
        return pltpu.make_async_remote_copy(
            src_ref=rows,
            dst_ref=rows,
            send_sem=fan_send.at[way, piece],
            recv_sem=fan_recv.at[way, piece],
            device_id=(segment, partner),
            device_id_type=MESH,
        )

    def out_copy(side, way, piece):
        owner = core if side == 0 else 1 - core
        rows = rows_of(owner * 2 + ring_block(way), piece)
        return pltpu.make_async_copy(
            landed.at[rows, :], received.at[rows, :], out_sem.at[side, way, piece]
        )

    def gain_copy(slot, other):
        return pltpu.make_async_remote_copy(
            src_ref=gain_sum,
            dst_ref=gain_buf.at[slot],
            send_sem=gain_send.at[other - 1],
            recv_sem=gain_recv.at[slot],
            device_id=(segment, (member + other) % members),
            device_id_type=MESH,
        )

    def start_pairs(piece, carry):
        for way in range(2):
            pair_copy(way, piece).start()
        return carry

    side = 2 * quarter
    theirs = pl.ds(pl.multiple_of((1 - core) * side, side), side)
    ours = pl.ds(pl.multiple_of(core * side, side), side)
    part[theirs, :] = dot_nt(d_all[theirs, :], w_v[...]).astype(BF16)
    pl.semaphore_wait(barrier, members + 1)
    lax.fori_loop(0, chunks, start_pairs, 0)
    part[ours, :] = dot_nt(d_all[ours, :], w_v[...]).astype(BF16)

    @pl.when(is_end)
    def _():
        gain_sum[...] = jnp.zeros_like(gain_sum)

        def norm_rows(i, carry):
            at = piece_of(i)
            value = x_v[rows_of(owned, i), :].astype(F32)
            centred = value - jnp.mean(value, -1, keepdims=True)
            inv = lax.rsqrt(jnp.mean(centred * centred, -1, keepdims=True) + 1e-05)
            standard[at, :] = centred * inv
            spread[at, :] = jnp.broadcast_to(inv, (CHUNK, 128))
            return carry

        lax.fori_loop(0, chunks, norm_rows, 0)

    def reduce_step(way, piece):
        spot = place(way)
        at = piece_of(piece)
        pair_copy(way, piece).wait_recv()
        total = (
            part[rows_of(core * 2 + way, piece), :].astype(F32)
            + pair_buf[way, at, :].astype(F32)
        )

        @pl.when(spot == 0)
        def _():
            line_out[way, at, :] = total.astype(BF16)
            line_copy(way, piece).start()

        @pl.when(jnp.logical_and(spot > 0, spot < last))
        def _():
            line_copy(way, piece).wait_recv()
            line_out[way, at, :] = (total + line_buf[way, at, :].astype(F32)).astype(BF16)
            line_copy(way, piece).start()

        @pl.when(spot == last)
        def _():
            line_copy(way, piece).wait_recv()
            d_normed = total + line_buf[way, at, :].astype(F32)
            unit = standard[at, :]
            scaled = d_normed * gain_ref[...]
            first_mean = jnp.mean(scaled, -1, keepdims=True)
            second_mean = jnp.mean(scaled * unit, -1, keepdims=True)
            inv = spread[at, :][:, :1]
            d_input[at, :] = (
                g_v[rows_of(owned, piece), :].astype(F32) + inv * (scaled - first_mean - unit * second_mean)
            ).astype(BF16)
            shift_copy(way, piece).start()
            gain_sum[...] += jnp.sum(d_normed * unit, 0, keepdims=True)

            @pl.when(piece == chunks - 1)
            def _():
                slot = jnp.where(chip == last, 2, 0) + core
                for other in range(1, members):
                    gain_copy(slot, other).start()

    def gather_step(way, piece):
        ring_copy(way, piece).wait_recv()

        @pl.when(place(way) < last)
        def _():
            ring_copy(way, piece).start()

        fan_copy(way, piece).start()
        out_copy(0, way, piece).start()

    steps = chunks + LAG * (2 * last + 1)

    wide_pieces = width // BLK
    tall_pieces = (cols + units) // BLK
    grad_start = jnp.where(is_end, GRAD_AT_END, GRAD_AT_MIDDLE)

    def grad_step(piece):
        @pl.when(jnp.logical_and(piece >= 0, piece < wide_pieces))
        def _():
            at = pl.ds(pl.multiple_of(piece * BLK, BLK), BLK)
            value = dot_tn(normed[:, at], d_all[...]).astype(BF16)
            for i in range(3):
                grad_qkv[0, i, at, :] = value[:, i * cols : (i + 1) * cols]
            grad_up[0, at, :] = value[:, 3 * cols :]

        @pl.when(piece == wide_pieces)
        def _():
            grad_out[...] = dot_tn(hidden[:, :cols], g_v[...]).astype(BF16)

        @pl.when(jnp.logical_and(piece > wide_pieces, piece < wide_pieces + tall_pieces))
        def _():
            spot = piece - wide_pieces
            at = pl.ds(pl.multiple_of(spot * BLK, BLK), BLK)
            down_at = pl.ds(pl.multiple_of(spot * BLK - cols, BLK), BLK)
            grad_down[down_at, :] = dot_tn(hidden[:, at], g_v[...]).astype(BF16)

    def slot(k, carry):
        for way in range(2):
            piece = k - LAG * place(way)

            @pl.when(jnp.logical_and(piece >= 0, piece < chunks))
            def _():
                reduce_step(way, piece)

        for way in range(2):
            piece = k - LAG * (last + 1 + place(way))

            @pl.when(jnp.logical_and(piece >= 0, piece < chunks))
            def _():
                gather_step(way, piece)

        grad_step(k - grad_start)
        return carry

    lax.fori_loop(0, steps, slot, 0)

    def finish(piece, carry):
        for way in range(2):
            fan_arrival(way, piece).wait_recv()
            out_copy(1, way, piece).start()
        return carry

    lax.fori_loop(0, chunks, finish, 0)

    owners = (0, 1, members - 2, members - 1)
    total = jnp.zeros_like(gain_sum[...])
    for slot_index, owner in enumerate(owners):

        @pl.when(member != owner)
        def _():
            gain_copy(slot_index, 1).wait_recv()

        @pl.when(member == owner)
        def _():
            gain_buf[slot_index] = gain_sum[...]

        total = total + gain_buf[slot_index]
    gain_out[...] = total

    def settle(piece, carry):
        for way in range(2):
            pair_copy(way, piece).wait_send()
            fan_copy(way, piece).wait_send()
            out_copy(0, way, piece).wait()
            out_copy(1, way, piece).wait()

            @pl.when(place(way) < last)
            def _():
                line_copy(way, piece).wait_send()
                ring_copy(way, piece).wait_send()

            @pl.when(place(way) == last)
            def _():
                shift_copy(way, piece).wait_send()

        return carry

    lax.fori_loop(0, chunks, settle, 0)

    @pl.when(is_end)
    def _():
        for other in range(1, members):
            gain_copy(0, other).wait_send()


def section(sections, members, x, g, gain, qkv, out, up, down, scale, near, valid, patch):
    tokens, width = x.shape
    cols = out.shape[1]
    units = down.shape[1]
    wide = 3 * cols + units
    tall = cols + units
    quarter = tokens // 4
    chunks = quarter // CHUNK
    smem = pl.BlockSpec(memory_space=pltpu.SMEM)
    vmem = pl.BlockSpec(memory_space=pltpu.VMEM)
    hbm = pl.BlockSpec(memory_space=pl.ANY)
    shape = jax.ShapeDtypeStruct
    dma = pltpu.SemaphoreType.DMA
    return pl.pallas_call(
        functools.partial(section_kernel, sections, members),
        out_shape=(
            shape((tokens, width), BF16),
            shape((1, width), F32),
            shape((1, 2), F32),
            shape(qkv.shape, BF16),
            shape((cols, width), BF16),
            shape(up.shape, BF16),
            shape((units, width), BF16),
        ),
        in_specs=[smem, smem, smem, smem, vmem, hbm, hbm, hbm, hbm, hbm, hbm],
        out_specs=[hbm, vmem, smem, vmem, vmem, vmem, vmem],
        scratch_shapes=[
            pltpu.VMEM((tokens, width), BF16),
            pltpu.VMEM((tokens, width), BF16),
            pltpu.VMEM((width, wide), BF16),
            pltpu.VMEM((tall, width), BF16),
            pltpu.VMEM((tokens, width), BF16),
            pltpu.VMEM((tokens, wide), F32),
            pltpu.VMEM((tokens, tall), F32),
            pltpu.VMEM((2, tokens, cols), BF16),
            pltpu.VMEM((tokens, cols), BF16),
            pltpu.VMEM((tokens, cols), BF16),
            pltpu.VMEM((2, tokens, cols), BF16),
            pltpu.VMEM((2, tokens, tokens), F32),
            pltpu.VMEM((2, tokens, tokens), F32),
            pltpu.VMEM((2 * tokens, tokens), BF16),
            pltpu.VMEM((2 * tokens, tokens), BF16),
            pltpu.VMEM((2, cols, 2 * tokens), BF16),
            pltpu.VMEM((tokens // BLK, 8, tokens), F32),
            pltpu.VMEM((tokens, tall), BF16),
            pltpu.VMEM((tokens, wide), BF16),
            pltpu.VMEM((tokens, width), BF16),
            pltpu.VMEM((2, quarter, width), BF16),
            pltpu.VMEM((2, quarter, width), BF16),
            pltpu.VMEM((2, quarter, width), BF16),
            pltpu.VMEM((quarter, width), BF16),
            pltpu.VMEM((quarter, width), F32),
            pltpu.VMEM((quarter, 128), F32),
            pltpu.VMEM((tokens, width), BF16),
            pltpu.VMEM((1, width), F32),
            pltpu.VMEM((4, 1, width), F32),
            dma((8,)),
            dma((2, chunks)),
            dma((2, chunks)),
            dma((2, chunks)),
            dma((2, chunks)),
            dma((chunks,)),
            dma((2, chunks)),
            dma((2, chunks)),
            dma((2, chunks)),
            dma((2, chunks)),
            dma((members - 1,)),
            dma((4,)),
            dma((2, 2, chunks)),
        ],
        compiler_params=pltpu.CompilerParams(
            collective_id=0, has_side_effects=True, vmem_limit_bytes=48 * 1024 * 1024
        ),
        name="section",
    )(
        patch,
        near.transpose(1, 2, 0),
        valid.transpose(1, 2, 0),
        scale,
        gain,
        x,
        g,
        qkv,
        out[0],
        up,
        down[0],
    )


def shards(sections, members, *arrays):
    received, gain_grad, grad_scale, grad_qkv, grad_out, grad_up, grad_down = section(
        sections, members, *arrays
    )
    return (
        received,
        grad_qkv,
        grad_out[None],
        grad_up,
        grad_down[None],
        gain_grad,
        grad_scale,
    )


def solution(mesh):
    placed = (
        P("segment", None),
        P("segment", None),
        P("segment", None),
        P("segment", None, None, "tp"),
        P("segment", "tp", None),
        P("segment", None, "tp"),
        P("segment", "tp", None),
        P("segment", "tp"),
        P(),
        P(),
        P("segment"),
    )
    return jax.shard_map(
        functools.partial(shards, mesh.shape["segment"], mesh.shape["tp"]),
        mesh=mesh,
        in_specs=placed,
        out_specs=(
            P("segment", None),
            P("segment", None, None, "tp"),
            P("segment", "tp", None),
            P("segment", None, "tp"),
            P("segment", "tp", None),
            P("segment", None),
            P("segment", "tp"),
        ),
        check_vma=False,
    )
```

time: 72 us -> 61.5 us (0.85)
  Pallas kernels: 64.8 us -> 49.6 us
  local copies, waits for them, and re-layouts: 5.63 us -> 9.71 us
    pallas_call x2 -> x1, Pallas kernels: 64.8 us -> 49.6 us  [section(): pl.pallas_call(functools.partial(section_kernel, sections, members), out_...]
    unnamed x14 -> x19, local copies, waits for them, and re-layouts: 5.63 us -> 9.71 us
where the time goes in v3:
time: 61.5 us; the launch traced here: 60.6 us
  Pallas kernels  49.6 us (81%)
  local copies, waits for them, and re-layouts  9.71 us (16%)
  between operations  1.33 us (2%)
    pallas_call x1, Pallas kernels, section(): pl.pallas_call(functools.partial(section_kernel, sections, members), out_...  49.6 us
    unnamed x19, local copies, waits for them, and re-layouts  9.71 us

profile of v3, /device:TPU:1, one launch (start us, length us, event | category | flops | bytes accessed | tf_op | source)
XLA Modules:
  0.0 60.6 jit_solution(636781366339449249)
XLA Ops:
  0.6 0.0 copy-start.2
  1.3 0.0 copy-start.5
  1.3 0.0 copy-done.2
  1.3 0.6 %copy-done.5 = f32[1,2]{1,0:T(1,128)S(1)} copy-done((f32[1,2]{1,0:T(1,128)S(1)}, f32[1,2]{1,0:T(1,128)}, u32[]{:S(2)}) %copy-start.5) | copy-done | bytes 32
  2.0 0.0 copy-start
  2.0 1.1 %copy-done = bf16[1,3,1024,128]{3,2,1,0:T(8,128)(2,1)S(1)} copy-done((bf16[1,3,1024,128]{3,2,1,0:T(8,128)(2,1)S(1)}, bf16[1,3,1024,128]{3,2,1,0:T(8,128)(2,1)}, u32[]{:S(2)}) %copy-start) | copy-done | bytes 786456
  3.1 0.0 copy-start.1
  3.1 0.9 %copy-done.1 = bf16[1,128,1024]{2,1,0:T(8,128)(2,1)S(1)} copy-done((bf16[1,128,1024]{2,1,0:T(8,128)(2,1)S(1)}, bf16[1,128,1024]{2,1,0:T(8,128)(2,1)}, u32[]{:S(2)}) %copy-start.1) | copy-done | bytes 262168
  4.0 0.0 copy-start.3
  4.0 0.7 %copy-done.3 = s32[32,4,4]{0,2,1:T(4,128)S(1)} copy-done((s32[32,4,4]{0,2,1:T(4,128)S(1)}, s32[32,4,4]{0,2,1:T(4,128)}, u32[]{:S(2)}) %copy-start.3) | copy-done | bytes 2072
  4.7 0.0 copy-start.4
  4.7 0.7 %copy-done.4 = f32[1,1024]{1,0:T(1,128)S(1)} copy-done((f32[1,1024]{1,0:T(1,128)S(1)}, f32[1,1024]{1,0:T(1,128)}, u32[]{:S(2)}) %copy-start.4) | copy-done | bytes 4120
  5.4 49.6 %section.1 = (bf16[512,1024]{1,0:T(8,128)(2,1)S(1)}, f32[1,1024]{1,0:T(1,128)S(1)}, f32[1,2]{1,0:T(1,128)S(1)}, bf16[1,3,1024,128]{3,2,1,0:T(8,128)(2,1)S(1)}, b...) custom-call(s32[1]{0:T(128)S(6)} %copy.25.patch_ref, ...), custom_call_target="tpu_custom_call" | custom-call | tf_op jit(solution)/shard_map/section/pallas_call | solution.py:548
  55.0 1.0 %copy.26 = bf16[512,1024]{1,0:T(8,128)(2,1)} copy(bf16[512,1024]{1,0:T(8,128)(2,1)S(1)} %get-tuple-element.28) | data formatting | bytes 2097152
  56.0 0.9 %copy.27 = bf16[1,3,1024,128]{3,2,1,0:T(8,128)(2,1)} copy(bf16[1,3,1024,128]{3,2,1,0:T(8,128)(2,1)S(1)} %get-tuple-element.29) | data formatting | bytes 1572864
  56.9 0.7 %copy.28 = bf16[1,128,1024]{2,1,0:T(8,128)(2,1)} copy(bf16[1,128,1024]{2,1,0:T(8,128)(2,1)S(1)} %bitcast.8) | data formatting | bytes 524288
  57.6 1.0 %copy.29 = bf16[1,1024,512]{2,1,0:T(8,128)(2,1)} copy(bf16[1,1024,512]{2,1,0:T(8,128)(2,1)S(1)} %get-tuple-element.31) | data formatting | bytes 2097152
  58.5 1.0 %copy.30 = bf16[1,512,1024]{2,1,0:T(8,128)(2,1)} copy(bf16[1,512,1024]{2,1,0:T(8,128)(2,1)S(1)} %bitcast.6) | data formatting | bytes 2097152
  59.5 0.6 copy.31
  60.1 0.5 copy.32
Async XLA Ops:
  0.6 0.7 %copy-start.2 = (s32[32,4,4]{0,2,1:T(4,128)S(1)}, s32[32,4,4]{0,2,1:T(4,128)}, u32[]{:S(2)}) copy-start(s32[32,4,4]{0,2,1:T(4,128)} %param.19) | copy-start | bytes 6148
  1.3 0.7 %copy-start.5 = (f32[1,2]{1,0:T(1,128)S(1)}, f32[1,2]{1,0:T(1,128)}, u32[]{:S(2)}) copy-start(f32[1,2]{1,0:T(1,128)} %scale_ref.1) | copy-start | bytes 28
  2.0 1.1 %copy-start = (bf16[1,3,1024,128]{3,2,1,0:T(8,128)(2,1)S(1)}, bf16[1,3,1024,128]{3,2,1,0:T(8,128)(2,1)}, u32[]{:S(2)}) copy-start(bf16[1,3,1024,128]{3,2,1,0:T(8,128)(2,1)} %qkv_hbm.1) | copy-start | bytes 2359300
  3.1 0.9 %copy-start.1 = (bf16[1,128,1024]{2,1,0:T(8,128)(2,1)S(1)}, bf16[1,128,1024]{2,1,0:T(8,128)(2,1)}, u32[]{:S(2)}) copy-start(bf16[1,128,1024]{2,1,0:T(8,128)(2,1)} %param.15) | copy-start | bytes 786436
  4.0 0.7 %copy-start.3 = (s32[32,4,4]{0,2,1:T(4,128)S(1)}, s32[32,4,4]{0,2,1:T(4,128)}, u32[]{:S(2)}) copy-start(s32[32,4,4]{0,2,1:T(4,128)} %param.20) | copy-start | bytes 6148
  4.7 0.7 %copy-start.4 = (f32[1,1024]{1,0:T(1,128)S(1)}, f32[1,1024]{1,0:T(1,128)}, u32[]{:S(2)}) copy-start(f32[1,1024]{1,0:T(1,128)} %gain_ref.1) | copy-start | bytes 12292

commit v4 on v3

--- a/solution.py
+++ b/solution.py
@@ -39,11 +39,11 @@
 def section_kernel(
     sections,
     members,
-    patch_ref,
-    near_ref,
-    valid_ref,
-    scale_ref,
-    gain_ref,
+    patch_hbm,
+    near_hbm,
+    valid_hbm,
+    scale_hbm,
+    gain_hbm,
     x_hbm,
     g_hbm,
     qkv_hbm,
@@ -86,6 +86,11 @@
     landed,
     gain_sum,
     gain_buf,
+    patch_ref,
+    near_ref,
+    valid_ref,
+    scale_ref,
+    gain_ref,
     in_sem,
     pair_send,
     pair_recv,
@@ -142,8 +147,17 @@
         pltpu.make_async_copy(up_hbm.at[0], w_v.at[:, pl.ds(3 * cols, units)], in_sem.at[6]),
         pltpu.make_async_copy(down_hbm, v_v.at[pl.ds(cols, units), :], in_sem.at[7]),
     ]
-    for load in loads:
+    small = [
+        pltpu.make_async_copy(patch_hbm, patch_ref, in_sem.at[8]),
+        pltpu.make_async_copy(near_hbm, near_ref, in_sem.at[9]),
+        pltpu.make_async_copy(valid_hbm, valid_ref, in_sem.at[10]),
+        pltpu.make_async_copy(scale_hbm, scale_ref, in_sem.at[11]),
+        pltpu.make_async_copy(gain_hbm, gain_ref, in_sem.at[12]),
+    ]
+    for load in loads[:1] + small + loads[1:]:
         load.start()
+    for load in small:
+        load.wait()
 
     patch = patch_ref[0]
     for b in range(blocks):
@@ -238,8 +252,9 @@
 
     zero = jnp.zeros((ROWS, tokens), F32)
     sums = lax.fori_loop(0, tokens // ROWS, both_rows, (zero, zero))
-    for h in range(2):
-        grad_scale_ref[0, h] = jnp.sum(sums[h])
+    grad_scale_ref[...] = jnp.where(
+        lax.broadcasted_iota(jnp.int32, (1, 2), 1) == 0, jnp.sum(sums[0]), jnp.sum(sums[1])
+    )
 
     first = lax.broadcasted_iota(jnp.int32, (tokens, cols), 1) < head
     hidden[:, :cols] = jnp.where(
@@ -540,9 +555,8 @@
     tall = cols + units
     quarter = tokens // 4
     chunks = quarter // CHUNK
-    smem = pl.BlockSpec(memory_space=pltpu.SMEM)
     vmem = pl.BlockSpec(memory_space=pltpu.VMEM)
-    hbm = pl.BlockSpec(memory_space=pl.ANY)
+    hbm = pl.BlockSpec(memory_space=pltpu.HBM)
     shape = jax.ShapeDtypeStruct
     dma = pltpu.SemaphoreType.DMA
     return pl.pallas_call(
@@ -556,8 +570,8 @@
             shape(up.shape, BF16),
             shape((units, width), BF16),
         ),
-        in_specs=[smem, smem, smem, smem, vmem, hbm, hbm, hbm, hbm, hbm, hbm],
-        out_specs=[hbm, vmem, smem, vmem, vmem, vmem, vmem],
+        in_specs=[hbm] * 11,
+        out_specs=[vmem] * 7,
         scratch_shapes=[
             pltpu.VMEM((tokens, width), BF16),
             pltpu.VMEM((tokens, width), BF16),
@@ -588,7 +602,12 @@
             pltpu.VMEM((tokens, width), BF16),
             pltpu.VMEM((1, width), F32),
             pltpu.VMEM((4, 1, width), F32),
-            dma((8,)),
+            pltpu.SMEM(patch.shape, jnp.int32),
+            pltpu.SMEM((4, 4, near.shape[0]), jnp.int32),
+            pltpu.SMEM((4, 4, near.shape[0]), jnp.int32),
+            pltpu.SMEM((1, 2), F32),
+            pltpu.VMEM((1, width), F32),
+            dma((13,)),
             dma((2, chunks)),
             dma((2, chunks)),
             dma((2, chunks)),
@@ -621,9 +640,40 @@
     )
 
 
+def place_kernel(*refs):
+    count = (len(refs) - 1) // 2
+    sems = refs[-1]
+    refs[count - 1 + count][...] = refs[count - 1][...]
+    copies = [
+        pltpu.make_async_copy(refs[i], refs[count + i], sems.at[i]) for i in range(count - 1)
+    ]
+    for copy in copies:
+        copy.start()
+    for copy in copies:
+        copy.wait()
+
+
+def placed_results(*arrays):
+    vmem = pl.BlockSpec(memory_space=pltpu.VMEM)
+    hbm = pl.BlockSpec(memory_space=pltpu.HBM)
+    count = len(arrays)
+    return pl.pallas_call(
+        place_kernel,
+        out_shape=tuple(jax.ShapeDtypeStruct(a.shape, a.dtype) for a in arrays),
+        in_specs=[vmem] * count,
+        out_specs=[hbm] * (count - 1) + [vmem],
+        scratch_shapes=[pltpu.SemaphoreType.DMA((count - 1,))],
+        compiler_params=pltpu.CompilerParams(vmem_limit_bytes=16 * 1024 * 1024),
+        name="placed_results",
+    )(*arrays)
+
+
 def shards(sections, members, *arrays):
     received, gain_grad, grad_scale, grad_qkv, grad_out, grad_up, grad_down = section(
         sections, members, *arrays
+    )
+    received, grad_qkv, grad_out, grad_up, grad_down, gain_grad, grad_scale = placed_results(
+        received, grad_qkv, grad_out, grad_up, grad_down, gain_grad, grad_scale
     )
     return (
         received,

time: 61.5 us -> 57 us (0.927)
  local copies, waits for them, and re-layouts: 9.71 us -> 4.12 us
  Pallas kernels: 49.6 us -> 50.7 us
    unnamed x19 -> x12, local copies, waits for them, and re-layouts: 9.71 us -> 4.12 us
    pallas_call x0 -> x1, Pallas kernels: none -> 2.57 us  [placed_results(): pl.pallas_call(place_kernel, out_shape=tuple((jax.ShapeDtypeStruct(a.shap...]
    pallas_call x1, Pallas kernels: 49.6 us -> 48.1 us  [section(): pl.pallas_call(functools.partial(section_kernel, sections, members), out_...]
where the time goes in v4:
time: 57 us; the launch traced here: 56.1 us
  Pallas kernels  50.7 us (89%)
  local copies, waits for them, and re-layouts  4.12 us (7%)
  between operations  1.32 us (2%)
    pallas_call x1, Pallas kernels, section(): pl.pallas_call(functools.partial(section_kernel, sections, members), out_...  48.1 us
    unnamed x12, local copies, waits for them, and re-layouts  4.12 us
    pallas_call x1, Pallas kernels, placed_results(): pl.pallas_call(place_kernel, out_shape=tuple((jax.ShapeDtypeStruct(a.shap...  2.57 us

profile of v4, /device:TPU:1, one launch (start us, length us, event | category | flops | bytes accessed | tf_op | source)
XLA Modules:
  0.0 56.1 jit_solution(5186860870595599797)
XLA Ops:
  0.6 0.0 copy-start.2
  1.3 0.0 copy-start.5
  1.3 0.0 copy-done.2
  1.3 0.6 %copy-done.5 = f32[1,2]{1,0:T(1,128)S(1)} copy-done((f32[1,2]{1,0:T(1,128)S(1)}, f32[1,2]{1,0:T(1,128)}, u32[]{:S(2)}) %copy-start.5) | copy-done | bytes 32
  2.0 0.0 copy-start
  2.0 1.1 %copy-done = bf16[1,3,1024,128]{3,2,1,0:T(8,128)(2,1)S(1)} copy-done((bf16[1,3,1024,128]{3,2,1,0:T(8,128)(2,1)S(1)}, bf16[1,3,1024,128]{3,2,1,0:T(8,128)(2,1)}, u32[]{:S(2)}) %copy-start) | copy-done | bytes 786456
  3.1 0.0 copy-start.1
  3.1 0.9 %copy-done.1 = bf16[1,128,1024]{2,1,0:T(8,128)(2,1)S(1)} copy-done((bf16[1,128,1024]{2,1,0:T(8,128)(2,1)S(1)}, bf16[1,128,1024]{2,1,0:T(8,128)(2,1)}, u32[]{:S(2)}) %copy-start.1) | copy-done | bytes 262168
  4.0 0.0 copy-start.3
  4.0 0.7 %copy-done.3 = s32[32,4,4]{0,2,1:T(4,128)S(1)} copy-done((s32[32,4,4]{0,2,1:T(4,128)S(1)}, s32[32,4,4]{0,2,1:T(4,128)}, u32[]{:S(2)}) %copy-start.3) | copy-done | bytes 2072
  4.7 0.0 copy-start.4
  4.7 0.7 %copy-done.4 = f32[1,1024]{1,0:T(1,128)S(1)} copy-done((f32[1,1024]{1,0:T(1,128)S(1)}, f32[1,1024]{1,0:T(1,128)}, u32[]{:S(2)}) %copy-start.4) | copy-done | bytes 4120
  5.4 48.1 %section.1 = (bf16[512,1024]{1,0:T(8,128)(2,1)S(1)}, f32[1,1024]{1,0:T(1,128)S(1)}, f32[1,2]{1,0:T(1,128)S(1)}, bf16[1,3,1024,128]{3,2,1,0:T(8,128)(2,1)S(1)}, b...) custom-call(s32[1]{0:T(128)S(6)} %copy.18.patch_hbm, ...), custom_call_target="tpu_custom_call" | custom-call | tf_op jit(solution)/shard_map/section/pallas_call | solution.py:562
  53.6 2.6 %placed_results.1 = (bf16[512,1024]{1,0:T(8,128)(2,1)}, bf16[1,3,1024,128]{3,2,1,0:T(8,128)(2,1)}, bf16[128,1024]{1,0:T(8,128)(2,1)}, bf16[1,1024,512]{2,1,0:T(8...) custom-call(bf16[512,1024]{1,0:T(8,128)(2,1)S(1)} %get-tuple-element.21.refs_0_, ...), custom_call_target="tpu_custom_call" | custom-call | tf_op jit(solution)/shard_map/placed_results/pallas_call | solution.py:660
Async XLA Ops:
  0.6 0.7 %copy-start.2 = (s32[32,4,4]{0,2,1:T(4,128)S(1)}, s32[32,4,4]{0,2,1:T(4,128)}, u32[]{:S(2)}) copy-start(s32[32,4,4]{0,2,1:T(4,128)} %param.19) | copy-start | bytes 6148
  1.3 0.7 %copy-start.5 = (f32[1,2]{1,0:T(1,128)S(1)}, f32[1,2]{1,0:T(1,128)}, u32[]{:S(2)}) copy-start(f32[1,2]{1,0:T(1,128)} %scale_hbm.1) | copy-start | bytes 28
  2.0 1.1 %copy-start = (bf16[1,3,1024,128]{3,2,1,0:T(8,128)(2,1)S(1)}, bf16[1,3,1024,128]{3,2,1,0:T(8,128)(2,1)}, u32[]{:S(2)}) copy-start(bf16[1,3,1024,128]{3,2,1,0:T(8,128)(2,1)} %qkv_hbm.1) | copy-start | bytes 2359300
  3.1 0.9 %copy-start.1 = (bf16[1,128,1024]{2,1,0:T(8,128)(2,1)S(1)}, bf16[1,128,1024]{2,1,0:T(8,128)(2,1)}, u32[]{:S(2)}) copy-start(bf16[1,128,1024]{2,1,0:T(8,128)(2,1)} %param.15) | copy-start | bytes 786436
  4.0 0.7 %copy-start.3 = (s32[32,4,4]{0,2,1:T(4,128)S(1)}, s32[32,4,4]{0,2,1:T(4,128)}, u32[]{:S(2)}) copy-start(s32[32,4,4]{0,2,1:T(4,128)} %param.20) | copy-start | bytes 6148
  4.7 0.7 %copy-start.4 = (f32[1,1024]{1,0:T(1,128)S(1)}, f32[1,1024]{1,0:T(1,128)}, u32[]{:S(2)}) copy-start(f32[1,1024]{1,0:T(1,128)} %gain_hbm.1) | copy-start | bytes 12292
